TPU v7x, 256 devices: a whole 4x4x8 slice. The times are simulated.
256 devices in a mesh: dp: 2 (over z_lo), node: 16 (over x, z_hi), local: 8 (over y, core).
Axes of the slice: x: 4, y: 4, z: 8 (z_hi: 4, z_lo: 2; z = z_hi * 2 + z_lo), core: 2. Of those that a mesh axis runs over, the one named last changes fastest.
Arguments:
- tokens_in: bfloat16 [2, 16, 64, 16, 3584], P('dp', 'node'), may hold values from -6 to 6
- grad_rows: bfloat16 [2, 16, 64, 16, 3584], P('dp', 'node'), may hold values from -6 to 6
- combine_weights: float32 [2, 16, 64, 16], P('dp', 'node'), may hold values from 0.05 to 1
- live_counts: int32 [2, 16, 16], P('dp', 'node'), may hold values from 0 to 64, as said below
- w_gate: bfloat16 [16, 3584, 2048], P('node', None, 'local'), may hold values from -0.09375 to 0.09375
- w_up: bfloat16 [16, 3584, 2048], P('node', None, 'local'), may hold values from -0.09375 to 0.09375
- w_down: bfloat16 [16, 3584, 2048], P('node', None, 'local'), may hold values from -0.125 to 0.125
Outputs:
- d_tokens: bfloat16 [2, 16, 64, 16, 3584], P('dp', 'node', 'local')
- grad_gate: bfloat16 [16, 3584, 2048], P('node', 'dp', 'local')
- grad_up: bfloat16 [16, 3584, 2048], P('node', 'dp', 'local')
- grad_down: bfloat16 [16, 3584, 2048], P('node', 'dp', 'local')
Inputs may be any that keep to these rules, and one draw needn't show every extreme that they name: `live_counts`: each replica has some source and expert pair with all 64 slots live; loads differ strongly between experts.
All inputs are finite; a program needn't handle non-finite values.
Results may differ from a plain program's by a relative error of at most 0.019.
Values may be sent and summed in bfloat16 or wider, within the bound.
A program may use at most 128 MiB of HBM per device.

v0:
```python
import jax
import jax.numpy as jnp
from jax import lax
from jax.sharding import PartitionSpec as P


def on_device(tokens_in, grad_rows, combine_weights, live_counts, w_gate, w_up, w_down):
    slot_count = tokens_in.shape[2]
    node_count = tokens_in.shape[3]
    feature_width = tokens_in.shape[4]
    gate_weight = w_gate[0]
    up_weight = w_up[0]
    down_weight = w_down[0]
    hid_local = gate_weight.shape[1]
    live_mask = (
        lax.broadcasted_iota(jnp.int32, (slot_count, node_count), 0) < live_counts[0, 0][None, :]
    ).astype(jnp.float32)
    scaled_rows = (
        grad_rows[0, 0].astype(jnp.float32) * (combine_weights[0, 0] * live_mask)[:, :, None]
    ).astype(jnp.bfloat16)
    scaled_rows = scaled_rows.reshape(slot_count * node_count, feature_width)
    flat_tokens = tokens_in[0, 0].reshape(slot_count * node_count, feature_width)
    gate_pre = jnp.dot(flat_tokens, gate_weight, preferred_element_type=jnp.float32)
    up_pre = jnp.dot(flat_tokens, up_weight, preferred_element_type=jnp.float32)
    sigmoid_gate = jax.nn.sigmoid(gate_pre)
    activated = gate_pre * sigmoid_gate
    hidden = (activated * up_pre).astype(jnp.bfloat16)
    hidden_grad = jnp.dot(scaled_rows, down_weight, preferred_element_type=jnp.float32)
    gate_grad = (
        hidden_grad * up_pre * sigmoid_gate * (1.0 + gate_pre * (1.0 - sigmoid_gate))
    ).astype(jnp.bfloat16)
    up_grad = (hidden_grad * activated).astype(jnp.bfloat16)
    joined_grad = jnp.concatenate((gate_grad, up_grad), axis=1)
    keep_rows = slot_count // lax.axis_size("local")
    total = lax.dot_general(
        gate_grad, gate_weight, (((1,), (1,)), ((), ())), preferred_element_type=jnp.float32
    )
    total = total + lax.dot_general(
        up_grad, up_weight, (((1,), (1,)), ((), ())), preferred_element_type=jnp.float32
    )
    summed = lax.psum_scatter(
        total.reshape(lax.axis_size("local") * keep_rows, node_count, feature_width).astype(
            jnp.bfloat16
        ),
        "local",
        scatter_dimension=0,
        tiled=True,
    )
    returned = lax.all_to_all(summed, "node", split_axis=1, concat_axis=1, tiled=True)
    d_tokens = returned[None, None]
    front = lax.dot_general(
        flat_tokens, joined_grad, (((0,), (0,)), ((), ())), preferred_element_type=jnp.float32
    )
    behind = lax.dot_general(
        scaled_rows, hidden, (((0,), (0,)), ((), ())), preferred_element_type=jnp.float32
    )
    weight_sums = lax.psum_scatter(
        jnp.concatenate((front, behind), axis=1).astype(jnp.bfloat16),
        "dp",
        scatter_dimension=0,
        tiled=True,
    ).astype(jnp.float32)
    grad_gate = weight_sums[:, :hid_local].astype(jnp.bfloat16)[None]
    grad_up = weight_sums[:, hid_local : 2 * hid_local].astype(jnp.bfloat16)[None]
    grad_down = weight_sums[:, 2 * hid_local :].astype(jnp.bfloat16)[None]
    return (d_tokens, grad_gate, grad_up, grad_down)


def solution(mesh):
    return jax.shard_map(
        on_device,
        mesh=mesh,
        in_specs=(
            P("dp", "node", None, None, None),
            P("dp", "node", None, None, None),
            P("dp", "node", None, None),
            P("dp", "node", None),
            P("node", None, "local"),
            P("node", None, "local"),
            P("node", None, "local"),
        ),
        out_specs=(
            P("dp", "node", "local", None, None),
            P("node", "dp", "local"),
            P("node", "dp", "local"),
            P("node", "dp", "local"),
        ),
        check_vma=False,
    )
```

profile of v0, /device:TPU:1, one launch (start us, length us, event | category | flops | bytes accessed | tf_op | source)
XLA Modules:
  0.0 213.1 jit_solution(1930631063470694649)
XLA Ops:
  7.2 0.0 copy-start
  7.2 0.0 reduce-scatter.7.cloned.1.call-start
  7.2 1.4 copy-done
  8.7 0.0 copy-start.2
  8.7 0.0 copy-start.6
  8.7 6.3 %fusion.4 = f32[1024,256]{0,1:T(8,128)} fusion(bf16[1024,3584]{1,0:T(8,128)(2,1)} %bitcast.56, bf16[1,3584,256]{2,1,0:T(8,128)(2,1)S(1)} %copy-done), kind=kOutput, calls=%fused_computation.10 | convolution fusion | flops 1879048192 | bytes 10223616 | tf_op jit(solution)/shard_map/dot_general | solution.py:23
  15.0 0.0 copy-done.2
  15.0 0.0 copy-done.6
  15.0 0.0 copy-start.4
  15.0 0.0 copy-start.5
  15.0 3.1 %fusion.7 = f32[1024,256]{0,1:T(8,128)} fusion(bf16[1024,3584]{1,0:T(8,128)(2,1)S(1)} %bitcast.58, bf16[1,3584,256]{2,1,0:T(8,128)(2,1)S(1)} %copy-done.2), kind=kOutput, calls=%fused_computation.13 | convolution fusion | flops 1879048192 | bytes 10223616 | tf_op jit(solution)/shard_map/dot_general | solution.py:24
  18.1 0.0 copy-done.4
  18.1 0.0 copy-done.5
  18.1 0.1 bitcast_select_fusion
  18.2 0.1 copy.27
  18.2 5.6 %multiply_convert_fusion = bf16[1,1,64,16,3584]{4,3,2,1,0:T(8,128)(2,1)S(1)} fusion(f32[64,16]{1,0:T(8,128)S(1)} %copy.27, bf16[1,1,64,16,3584]{4,3,2,1,0:T(8,128)(2,1)} %param.8), kind=kLoop, calls=%fused_computation.3 | loop fusion | flops 11010048 | bytes 14684160 | tf_op jit(solution)/shard_map/convert_element_type | solution.py:20
  23.8 4.5 %multiply_convert_fusion.2 = (bf16[1024,256]{0,1:T(8,128)(2,1)S(1)}, bf16[1024,256]{0,1:T(8,128)(2,1)S(1)}) fusion(f32[1024,256]{0,1:T(8,128)} %fusion.4, f32[1024,256]{0,1:T(8,128)} %fusion.7, bf16[1024,3584]{1,0:T(8,128)(2,1)S(1)} %bitcast.51, bf16[1,3584,256]{2,1,0:T(8,128)(2,1)} %param.13), kind=kOutput, calls=%fused_computation.21 | convolution fusion | flops 1882456064 | bytes 12320768 | tf_op jit(solution)/shard_map/dot_general | solution.py:28
  28.3 0.0 copy-start.3
  28.4 7.3 %fusion.2 = f32[1024,3584]{1,0:T(8,128)} fusion(bf16[1024,256]{0,1:T(8,128)(2,1)S(1)} %get-tuple-element.24, bf16[1,3584,256]{2,1,0:T(8,128)(2,1)S(1)} %copy-done), kind=kOutput, calls=%fused_computation.8 | convolution fusion | flops 1879048192 | bytes 17039360 | tf_op jit(solution)/shard_map/dot_general | solution.py:35
  35.7 0.0 copy-done.3
  35.7 7.5 %add_convert_fusion = bf16[1024,3584]{1,0:T(8,128)(2,1)S(1)} fusion(f32[1024,3584]{1,0:T(8,128)} %fusion.2, bf16[1024,256]{0,1:T(8,128)(2,1)S(1)} %get-tuple-element.23, bf16[1,3584,256]{2,1,0:T(8,128)(2,1)S(1)} %copy-done.3), kind=kOutput, calls=%fused_computation.2 | convolution fusion | flops 1886388224 | bytes 24379392 | tf_op jit(solution)/shard_map/dot_general | solution.py:38
  43.2 7.1 %copy.36 = bf16[8,8,16,3584]{3,1,2,0:T(8,128)(2,1)} copy(bf16[8,8,16,3584]{3,2,1,0:T(8,128)(2,1)S(1)} %bitcast.50) | data formatting | bytes 14680064
  50.4 0.0 reduce-scatter.7.cloned.1.call-update
  50.4 0.0 reduce-scatter.5.cloned.1.call-start
  50.4 0.1 copy.29
  50.5 0.1 squeeze.19
  50.6 0.1 iota.15
  50.7 0.1 lt.25
  50.8 5.5 %fusion = bf16[1024,3584]{1,0:T(8,128)(2,1)S(1)} fusion(f32[1024]{0:T(1024)S(1)} %compare_select_fusion, bf16[1,1,64,16,3584]{4,3,2,1,0:T(8,128)(2,1)} %param.8), kind=kLoop, calls=%fused_computation.1 | loop fusion | flops 11010048 | bytes 14684160 | tf_op jit(solution)/shard_map/convert_element_type | solution.py:20
  56.3 3.7 %convolution_convert_fusion.1 = bf16[3584,256]{0,1:T(8,128)(2,1)S(1)} fusion(bf16[1024,3584]{1,0:T(8,128)(2,1)S(1)} %fusion, f32[1024,256]{0,1:T(8,128)} %fusion.7, f32[1024,256]{0,1:T(8,128)} %fusion.4), kind=kOutput, calls=%fused_computation.7 | convolution fusion | flops 1881538560 | bytes 11272192 | tf_op jit(solution)/shard_map/dot_general | solution.py:54
  60.0 7.8 %fusion.1 = bf16[3584,512]{0,1:T(8,128)(2,1)S(1)} fusion(bf16[1024,3584]{1,0:T(8,128)(2,1)} %bitcast.57, bf16[1024,256]{0,1:T(8,128)(2,1)S(1)} %get-tuple-element.23, bf16[1024,256]{0,1:T(8,128)(2,1)S(1)} %get-tuple-element.24), kind=kOutput, calls=%fused_computation.6 | convolution fusion | flops 3762028544 | bytes 12058624 | tf_op jit(solution)/shard_map/dot_general | solution.py:51
  67.8 2.7 %pad_maximum_fusion = bf16[3584,768]{0,1:T(8,128)(2,1)} fusion(bf16[3584,256]{0,1:T(8,128)(2,1)S(1)} %convolution_convert_fusion.1, bf16[3584,512]{0,1:T(8,128)(2,1)S(1)} %fusion.1), kind=kLoop, calls=%fused_computation.5 | loop fusion | flops 11010048 | bytes 11010048 | tf_op jit(solution)/shard_map/concatenate | solution.py:58
  70.5 0.0 reduce-scatter.5.cloned.1.call-update
  70.6 33.2 %reduce-scatter.7.cloned.1.call-done = bf16[8,57344]{1,0:T(8,128)(2,1)} async-done(((bf16[64,57344]{1,0:T(8,128)(2,1)}), bf16[8,57344]{1,0:T(8,128)(2,1)}) %reduce-scatter.7.cloned.1.call-update) | async-done | bytes 917520
  103.8 0.0 copy-start.1
  103.8 9.4 %all-to-all-start = ((bf16[8,16,3584]{2,0,1:T(8,128)(2,1)}), bf16[8,16,3584]{2,0,1:T(8,128)(2,1)S(1)}, u32[]{:S(2)}, u32[]{:S(2)}) async-start(bf16[8,16,3584]{2,0,1:T(8,128)(2,1)} %bitcast.53), calls=%async_computation | async-start | bytes 1835008 | tf_op jit(solution)/shard_map/all_to_all | solution.py:49
  113.2 81.9 %reduce-scatter.5.cloned.1.call-done = bf16[1792,768]{0,1:T(8,128)(2,1)} async-done(((bf16[3584,768]{0,1:T(8,128)(2,1)}), bf16[1792,768]{0,1:T(8,128)(2,1)}) %reduce-scatter.5.cloned.1.call-update) | async-done | bytes 2752528 | tf_op jit(solution)/shard_map/reduce_scatter | solution.py:57
  195.1 3.3 %slice_bitcast_fusion = (bf16[1,1792,256]{1,2,0:T(8,128)(2,1)}, bf16[1,1792,256]{1,2,0:T(8,128)(2,1)}, bf16[1,1792,256]{1,2,0:T(8,128)(2,1)}) fusion(bf16[1792,768]{0,1:T(8,128)(2,1)} %reduce-scatter.5.cloned.1.call-done), kind=kLoop, calls=%fused_computation.25 | loop fusion | bytes 5505024 | tf_op jit(solution)/shard_map/broadcast_in_dim | solution.py:65
  198.4 2.2 %copy.31 = bf16[1,1792,256]{2,1,0:T(8,128)(2,1)} copy(bf16[1,1792,256]{1,2,0:T(8,128)(2,1)} %get-tuple-element.22) | data formatting | bytes 1835008
  200.6 2.2 %copy.32 = bf16[1,1792,256]{2,1,0:T(8,128)(2,1)} copy(bf16[1,1792,256]{1,2,0:T(8,128)(2,1)} %get-tuple-element.21) | data formatting | bytes 1835008
  202.8 2.2 %copy.33 = bf16[1,1792,256]{2,1,0:T(8,128)(2,1)} copy(bf16[1,1792,256]{1,2,0:T(8,128)(2,1)} %get-tuple-element.20) | data formatting | bytes 1835008
  205.1 0.0 all-to-all-done
  205.1 1.2 copy.30
  206.3 0.0 copy-done.1
  (3 shorter events, 0.0 us)
Async XLA Ops:
  7.2 1.5 copy-start
  7.2 96.6 %reduce-scatter.7.cloned.1.call-start = ((), (), s32[]{:S(2)}) async-start(), calls=%async_computation.4 | async-start | bytes 8257536
  8.7 6.3 %copy-start.2 = (bf16[1,3584,256]{2,1,0:T(8,128)(2,1)S(1)}, bf16[1,3584,256]{2,1,0:T(8,128)(2,1)}, u32[]{:S(2)}) copy-start(bf16[1,3584,256]{2,1,0:T(8,128)(2,1)} %param.12) | copy-start | bytes 5505028
  8.7 6.3 %copy-start.6 = (bf16[1,1,64,16,3584]{4,3,2,1,0:T(8,128)(2,1)S(1)}, bf16[1,1,64,16,3584]{4,3,2,1,0:T(8,128)(2,1)}, u32[]{:S(2)}) copy-start(bf16[1,1,64,16,3584]{4,3,2,1,0:T(8,128)(2,1)} %param.7) | copy-start | bytes 22020100
  15.0 3.1 %copy-start.4 = (f32[1,1,64,16]{2,3,1,0:T(8,128)S(1)}, f32[1,1,64,16]{2,3,1,0:T(8,128)}, u32[]{:S(2)}) copy-start(f32[1,1,64,16]{2,3,1,0:T(8,128)} %param.9) | copy-start | bytes 12292
  15.0 3.1 %copy-start.5 = (s32[1,1,16]{2,1,0:T(1,128)S(1)}, s32[1,1,16]{2,1,0:T(1,128)}, u32[]{:S(2)}) copy-start(s32[1,1,16]{2,1,0:T(1,128)} %param.10) | copy-start | bytes 196
  28.3 7.3 %copy-start.3 = (bf16[1,3584,256]{2,1,0:T(8,128)(2,1)S(1)}, bf16[1,3584,256]{2,1,0:T(8,128)(2,1)}, u32[]{:S(2)}) copy-start(bf16[1,3584,256]{2,1,0:T(8,128)(2,1)} %param.12) | copy-start | bytes 5505028
  50.4 144.7 %reduce-scatter.5.cloned.1.call-start = ((), (), s32[]{:S(2)}) async-start(), calls=%async_computation.3 | async-start | bytes 8257536 | tf_op jit(solution)/shard_map/reduce_scatter | solution.py:57
  103.8 102.5 %copy-start.1 = (bf16[1,3584,256]{2,1,0:T(8,128)(2,1)S(1)}, bf16[1,3584,256]{2,1,0:T(8,128)(2,1)}, u32[]{:S(2)}) copy-start(bf16[1,3584,256]{2,1,0:T(8,128)(2,1)} %param.11) | copy-start | bytes 5505028
  103.8 101.3 %all-to-all-start = ((bf16[8,16,3584]{2,0,1:T(8,128)(2,1)}), bf16[8,16,3584]{2,0,1:T(8,128)(2,1)S(1)}, u32[]{:S(2)}, u32[]{:S(2)}) async-start(bf16[8,16,3584]{2,0,1:T(8,128)(2,1)} %bitcast.53), calls=%async_computation | async-start | bytes 1835008 | tf_op jit(solution)/shard_map/all_to_all | solution.py:49
Sparse Core Ops, SparseCore 0:
  50.5 53.2 reduce-scatter.6
  106.3 88.7 reduce-scatter.4
where the time goes:
time: 214 us; the launch traced here: 213 us
  waiting for transfers between devices  115 us (54%)
  matrix products  40.2 us (19%)
  local copies, waits for them, and re-layouts  20.2 us (9%)
  between operations  14.1 us (7%)
  other arithmetic  13.9 us (6%)
  starting transfers between devices  9.47 us (4%)
    reduce_scatter x1, waiting for transfers between devices, on_device(): lax.psum_scatter(jnp.concatenate((front, behind), axis=1).astype(jnp.bflo...  81.9 us
    unnamed x3, waiting for transfers between devices  33.2 us
    unnamed x20, local copies, waits for them, and re-layouts  16.5 us
    convert_element_type x2, other arithmetic, on_device(): scaled_rows = (grad_rows[0, 0].astype(jnp.float32) * (combine_weights[0,...  11.1 us
    all_to_all x1, starting transfers between devices, on_device(): lax.all_to_all(summed, 'node', split_axis=1, concat_axis=1, tiled=True)  9.39 us
    dot_general x1, matrix products, on_device(): lax.dot_general(flat_tokens, joined_grad, (((0,), (0,)), ((), ())), prefe...  7.78 us
    dot_general x1, matrix products, on_device(): lax.dot_general(up_grad, up_weight, (((1,), (1,)), ((), ())), preferred_e...  7.51 us
    dot_general x1, matrix products, on_device(): lax.dot_general(gate_grad, gate_weight, (((1,), (1,)), ((), ())), preferr...  7.33 us
  transfers between devices with their start and end apart: 3, of which 2 were waited for; matrix products, arithmetic and copies ran while one was open for 14% of the time, Pallas kernels for 0%

commit v1 on v0

v1 whole, which is shorter than its diff:
```python
import jax
import jax.numpy as jnp
from jax import lax
from jax.sharding import PartitionSpec as P

SWAP = [(0, 1), (1, 0)]


def on_device(tokens_in, grad_rows, combine_weights, live_counts, w_gate, w_up, w_down):
    slot_count = tokens_in.shape[2]
    node_count = tokens_in.shape[3]
    feature_width = tokens_in.shape[4]
    row_count = slot_count * node_count
    half = feature_width // 2
    gate_weight = w_gate[0]
    up_weight = w_up[0]
    down_weight = w_down[0]
    mine = lax.axis_index("dp")
    live_mask = (
        lax.broadcasted_iota(jnp.int32, (slot_count, node_count), 0) < live_counts[0, 0][None, :]
    ).astype(jnp.float32)
    scaled_rows = (
        grad_rows[0, 0].astype(jnp.float32) * (combine_weights[0, 0] * live_mask)[:, :, None]
    ).astype(jnp.bfloat16)
    scaled_rows = scaled_rows.reshape(row_count, feature_width)
    flat_tokens = tokens_in[0, 0].reshape(row_count, feature_width)
    gate_pre = jnp.dot(flat_tokens, gate_weight, preferred_element_type=jnp.float32)
    up_pre = jnp.dot(flat_tokens, up_weight, preferred_element_type=jnp.float32)
    sigmoid_gate = jax.nn.sigmoid(gate_pre)
    activated = gate_pre * sigmoid_gate
    hidden = (activated * up_pre).astype(jnp.bfloat16)
    hidden_grad = jnp.dot(scaled_rows, down_weight, preferred_element_type=jnp.float32)
    gate_grad = (
        hidden_grad * up_pre * sigmoid_gate * (1.0 + gate_pre * (1.0 - sigmoid_gate))
    ).astype(jnp.bfloat16)
    up_grad = (hidden_grad * activated).astype(jnp.bfloat16)

    def weight_grad(rows, grads):
        full = lax.dot_general(
            rows, grads, (((0,), (0,)), ((), ())), preferred_element_type=jnp.float32
        ).astype(jnp.bfloat16)
        keep = lax.dynamic_slice_in_dim(full, mine * half, half, 0)
        send = lax.dynamic_slice_in_dim(full, (1 - mine) * half, half, 0)
        return keep, lax.ppermute(send, "dp", SWAP)

    down_keep, down_got = weight_grad(scaled_rows, hidden)
    gate_keep, gate_got = weight_grad(flat_tokens, gate_grad)
    up_keep, up_got = weight_grad(flat_tokens, up_grad)

    total = lax.dot_general(
        gate_grad, gate_weight, (((1,), (1,)), ((), ())), preferred_element_type=jnp.float32
    )
    total = total + lax.dot_general(
        up_grad, up_weight, (((1,), (1,)), ((), ())), preferred_element_type=jnp.float32
    )
    summed = lax.psum_scatter(
        total.astype(jnp.bfloat16), "local", scatter_dimension=0, tiled=True
    )
    summed = lax.optimization_barrier(summed)
    summed = summed.reshape(-1, node_count, feature_width)
    returned = lax.all_to_all(summed, "node", split_axis=1, concat_axis=1, tiled=True)
    d_tokens = returned[None, None]

    def join(keep, got):
        return (keep.astype(jnp.float32) + got.astype(jnp.float32)).astype(jnp.bfloat16)[None]

    return (
        d_tokens,
        join(gate_keep, gate_got),
        join(up_keep, up_got),
        join(down_keep, down_got),
    )


def solution(mesh):
    return jax.shard_map(
        on_device,
        mesh=mesh,
        in_specs=(
            P("dp", "node", None, None, None),
            P("dp", "node", None, None, None),
            P("dp", "node", None, None),
            P("dp", "node", None),
            P("node", None, "local"),
            P("node", None, "local"),
            P("node", None, "local"),
        ),
        out_specs=(
            P("dp", "node", "local", None, None),
            P("node", "dp", "local"),
            P("node", "dp", "local"),
            P("node", "dp", "local"),
        ),
        check_vma=False,
    )
```

time: 214 us -> 163 us (0.76)
  waiting for transfers between devices: 115 us -> 55.3 us
  matrix products: 40.2 us -> 45.5 us
  local copies, waits for them, and re-layouts: 20.2 us -> 15 us
  other arithmetic: 13.9 us -> 19 us
  starting transfers between devices: 9.47 us -> 12.1 us
    reduce_scatter x1, waiting for transfers between devices: 81.9 us -> 27.9 us  [on_device(): lax.psum_scatter(total.astype(jnp.bfloat16), 'local', scatter_dimension=0...]
    unnamed x3 -> x1, waiting for transfers between devices: 33.2 us -> 0.02 us
    ppermute x0 -> x3, waiting for transfers between devices: none -> 27.4 us  [weight_grad(): return (keep, lax.ppermute(send, 'dp', SWAP))]
    unnamed x20 -> x28, local copies, waits for them, and re-layouts: 16.5 us -> 7.71 us
    broadcast_in_dim x0 -> x3, other arithmetic: none -> 7.65 us  [join(): (keep.astype(jnp.float32) + got.astype(jnp.float32)).astype(jnp.bfloat16)]
    dynamic_slice x0 -> x3, local copies, waits for them, and re-layouts: none -> 4.37 us  [weight_grad(): send = lax.dynamic_slice_in_dim(full, (1 - mine) * half, half, 0)]
    broadcast_in_dim x1 -> x0, local copies, waits for them, and re-layouts: 3.32 us -> none  [on_device(): grad_down = weight_sums[:, 2 * hid_local:].astype(jnp.bfloat16)[None]]
    ppermute x0 -> x3, starting transfers between devices: none -> 2.85 us  [weight_grad(): return (keep, lax.ppermute(send, 'dp', SWAP))]
  transfers between devices with their start and end apart: 3 -> 5, of which waited for: 2 -> 2; matrix products, arithmetic and copies ran while one was open for 14% -> 24% of each run, Pallas kernels for 0% -> 0%
where the time goes in v1:
time: 163 us; the launch traced here: 161 us
  waiting for transfers between devices  55.3 us (34%)
  matrix products  45.5 us (28%)
  other arithmetic  19 us (12%)
  local copies, waits for them, and re-layouts  15 us (9%)
  between operations  14.2 us (9%)
  starting transfers between devices  12.1 us (7%)
    reduce_scatter x1, waiting for transfers between devices, on_device(): lax.psum_scatter(total.astype(jnp.bfloat16), 'local', scatter_dimension=0...  27.9 us
    ppermute x3, waiting for transfers between devices, weight_grad(): return (keep, lax.ppermute(send, 'dp', SWAP))  27.4 us
    dot_general x3, matrix products, weight_grad(): lax.dot_general(rows, grads, (((0,), (0,)), ((), ())), preferred_element_...  14.3 us
    convert_element_type x2, other arithmetic, on_device(): scaled_rows = (grad_rows[0, 0].astype(jnp.float32) * (combine_weights[0,...  11.3 us
    dot_general x1, matrix products, on_device(): lax.dot_general(up_grad, up_weight, (((1,), (1,)), ((), ())), preferred_e...  10.2 us
    all_to_all x1, starting transfers between devices, on_device(): lax.all_to_all(summed, 'node', split_axis=1, concat_axis=1, tiled=True)  9.25 us
    unnamed x28, local copies, waits for them, and re-layouts  7.71 us
    broadcast_in_dim x3, other arithmetic, join(): (keep.astype(jnp.float32) + got.astype(jnp.float32)).astype(jnp.bfloat16)  7.65 us
  transfers between devices with their start and end apart: 5, of which 2 were waited for; matrix products, arithmetic and copies ran while one was open for 24% of the time, Pallas kernels for 0%

profile of v1, /device:TPU:1, one launch (start us, length us, event | category | flops | bytes accessed | tf_op | source)
XLA Modules:
  0.0 161.2 jit_solution(15735687788138049189)
XLA Ops:
  7.2 0.0 copy-start
  7.2 0.0 reduce-scatter.2.cloned.1.call-start
  7.2 1.4 copy-done
  8.7 6.3 %fusion.5 = f32[1024,256]{1,0:T(8,128)} fusion(bf16[1024,3584]{1,0:T(8,128)(2,1)} %bitcast.62, bf16[1,3584,256]{2,1,0:T(8,128)(2,1)S(1)} %copy-done), kind=kOutput, calls=%fused_computation.13 | convolution fusion | flops 1879048192 | bytes 10223616 | tf_op jit(solution)/shard_map/dot_general | solution.py:27
  15.0 0.0 copy-done.2
  15.0 0.0 copy-done.6
  15.0 3.0 %fusion.8 = f32[1024,256]{1,0:T(8,128)} fusion(bf16[1024,3584]{1,0:T(8,128)(2,1)S(1)} %bitcast.65, bf16[1,3584,256]{2,1,0:T(8,128)(2,1)S(1)} %copy-done.6), kind=kOutput, calls=%fused_computation.16 | convolution fusion | flops 1879048192 | bytes 10223616 | tf_op jit(solution)/shard_map/dot_general | solution.py:28
  18.0 0.0 copy-done.8
  18.0 0.1 bitcast_select_fusion
  18.1 0.1 copy.18
  18.2 5.6 %multiply_convert_fusion = bf16[1,1,64,16,3584]{4,3,2,1,0:T(8,128)(2,1)S(1)} fusion(f32[64,16]{1,0:T(8,128)S(1)} %copy.18, bf16[1,1,64,16,3584]{4,3,2,1,0:T(8,128)(2,1)} %param.8), kind=kLoop, calls=%fused_computation.3 | loop fusion | flops 11010048 | bytes 14684160 | tf_op jit(solution)/shard_map/convert_element_type | solution.py:24
  23.8 4.4 %multiply_convert_fusion.2 = (bf16[1024,256]{1,0:T(8,128)(2,1)S(1)}, bf16[1024,256]{1,0:T(8,128)(2,1)S(1)}) fusion(f32[1024,256]{1,0:T(8,128)} %fusion.5, f32[1024,256]{1,0:T(8,128)} %fusion.8, bf16[1024,3584]{1,0:T(8,128)(2,1)S(1)} %bitcast.66, bf16[1,3584,256]{2,1,0:T(8,128)(2,1)} %param.13), kind=kOutput, calls=%fused_computation.22 | convolution fusion | flops 1882456064 | bytes 12320768 | tf_op jit(solution)/shard_map/dot_general | solution.py:32
  28.2 0.0 copy-start.7
  28.2 7.3 %fusion.3 = f32[1024,3584]{1,0:T(8,128)} fusion(bf16[1024,256]{1,0:T(8,128)(2,1)S(1)} %get-tuple-element.17, bf16[1,3584,256]{2,1,0:T(8,128)(2,1)S(1)} %copy-done), kind=kOutput, calls=%fused_computation.11 | convolution fusion | flops 1879048192 | bytes 17039360 | tf_op jit(solution)/shard_map/dot_general | solution.py:50
  35.5 10.2 %add_convert_fusion = bf16[1024,3584]{1,0:T(8,128)(2,1)} fusion(f32[1024,3584]{1,0:T(8,128)} %fusion.3, bf16[1024,256]{1,0:T(8,128)(2,1)S(1)} %get-tuple-element.16, bf16[1,3584,256]{2,1,0:T(8,128)(2,1)S(1)} %copy-done.7), kind=kOutput, calls=%fused_computation.2 | convolution fusion | flops 1886388224 | bytes 24379392 | tf_op jit(solution)/shard_map/dot_general | solution.py:53
  45.7 0.0 reduce-scatter.2.cloned.1.call-update
  45.8 5.4 %convolution_convert_fusion.2 = bf16[256,3584]{1,0:T(8,128)(2,1)S(1)} fusion(bf16[1024,256]{1,0:T(8,128)(2,1)S(1)} %get-tuple-element.17, bf16[1024,3584]{1,0:T(8,128)(2,1)} %bitcast.63), kind=kOutput, calls=%fused_computation.6 | convolution fusion | flops 1879965696 | bytes 9699328 | tf_op jit(solution)/shard_map/dot_general | solution.py:39
  51.2 1.1 dynamic-slice_bitcast_fusion.1
  52.2 0.5 copy-done.4
  52.7 2.5 %collective-permute-start = (bf16[1792,256]{0,1:T(8,128)(2,1)}, bf16[1792,256]{0,1:T(8,128)(2,1)}, u32[]{:S(2)}, u32[]{:S(2)}) collective-permute-start(bf16[1792,256]{0,1:T(8,128)(2,1)} %dynamic-slice_bitcast_fusion.1), channel_id=1, source_target_pairs={{0,128},{128,0},{1,129},{129,1},{2,130},{130,2},{3,131},{131,3},{4... | collective-permute-start | bytes 2752520 | tf_op jit(solution)/shard_map/ppermute | solution.py:44
  55.2 5.2 %convolution_convert_fusion.1 = bf16[256,3584]{1,0:T(8,128)(2,1)S(1)} fusion(bf16[1024,256]{1,0:T(8,128)(2,1)S(1)} %get-tuple-element.16, bf16[1024,3584]{1,0:T(8,128)(2,1)} %bitcast.64), kind=kOutput, calls=%fused_computation.5 | convolution fusion | flops 1879965696 | bytes 9699328 | tf_op jit(solution)/shard_map/dot_general | solution.py:39
  60.4 1.1 dynamic-slice_bitcast_fusion
  61.4 0.0 collective-permute-start.1
  61.5 0.1 copy.20
  61.5 0.1 squeeze.19
  61.6 0.1 iota.15
  61.7 0.1 lt.37
  61.8 5.7 %fusion = bf16[1024,3584]{1,0:T(8,128)(2,1)S(1)} fusion(f32[1024]{0:T(1024)S(1)} %compare_select_fusion, bf16[1,1,64,16,3584]{4,3,2,1,0:T(8,128)(2,1)} %param.8), kind=kLoop, calls=%fused_computation.1 | loop fusion | flops 11010048 | bytes 14684160 | tf_op jit(solution)/shard_map/convert_element_type | solution.py:24
  67.5 0.0 copy-done.3
  67.5 0.0 copy-done.10
  67.5 0.0 copy-done.11
  67.5 3.7 %convolution_convert_fusion = bf16[3584,256]{1,0:T(8,128)(2,1)} fusion(bf16[1024,3584]{1,0:T(8,128)(2,1)S(1)} %fusion, f32[1024,256]{1,0:T(8,128)S(1)} %copy-done.11, f32[1024,256]{1,0:T(8,128)S(1)} %copy-done.10), kind=kOutput, calls=%fused_computation.4 | convolution fusion | flops 1881538560 | bytes 11272192 | tf_op jit(solution)/shard_map/dot_general | solution.py:39
  71.3 27.9 %reduce-scatter.2.cloned.1.call-done = bf16[128,3584]{1,0:T(8,128)(2,1)} async-done(((bf16[1024,3584]{1,0:T(8,128)(2,1)}), bf16[128,3584]{1,0:T(8,128)(2,1)}) %reduce-scatter.2.cloned.1.call-update) | async-done | bytes 917520 | tf_op jit(solution)/shard_map/reduce_scatter | solution.py:56
  99.2 2.6 %copy.19 = bf16[8,16,3584]{2,0,1:T(8,128)(2,1)} copy(bf16[8,16,3584]{2,1,0:T(8,128)(2,1)} %bitcast.68) | data formatting | bytes 1835008 | tf_op jit(solution)/shard_map/reshape | solution.py:60
  101.8 9.3 %all-to-all-start = ((bf16[8,16,3584]{2,0,1:T(8,128)(2,1)}), bf16[8,16,3584]{2,0,1:T(8,128)(2,1)S(1)}, u32[]{:S(2)}, u32[]{:S(2)}) async-start(bf16[8,16,3584]{2,0,1:T(8,128)(2,1)} %copy.19), calls=%async_computation.1 | async-start | bytes 1835008 | tf_op jit(solution)/shard_map/all_to_all | solution.py:61
  111.0 2.3 %constant_dynamic-slice_fusion = bf16[1792,256]{1,0:T(8,128)(2,1)} fusion(bf16[3584,256]{1,0:T(8,128)(2,1)} %convolution_convert_fusion, s32[]{:T(128)S(6)} %select_n.5), kind=kLoop, calls=%fused_computation.34 | loop fusion | bytes 1835012 | tf_op jit(solution)/shard_map/dynamic_slice | solution.py:43
  113.3 0.4 collective-permute-start.2
  113.7 0.0 collective-permute-done
  113.7 2.3 %fusion.14 = bf16[1,1792,256]{1,2,0:T(8,128)(2,1)} fusion(bf16[1792,256]{0,1:T(8,128)(2,1)} %collective-permute-done, bf16[256,3584]{1,0:T(8,128)(2,1)S(1)} %copy-done.5, s32[]{:T(128)S(6)} %select_n.4), kind=kLoop, calls=%fused_computation.27 | loop fusion | flops 1835008 | bytes 2752516 | tf_op jit(solution)/shard_map/broadcast_in_dim | solution.py:65
  116.0 2.2 %copy.22 = bf16[1,1792,256]{2,1,0:T(8,128)(2,1)} copy(bf16[1,1792,256]{1,2,0:T(8,128)(2,1)} %fusion.14) | data formatting | bytes 1835008
  118.2 0.0 collective-permute-done.1
  118.2 2.7 %fusion.15 = bf16[1,1792,256]{1,2,0:T(8,128)(2,1)} fusion(bf16[1792,256]{0,1:T(8,128)(2,1)} %collective-permute-done.1, bf16[256,3584]{1,0:T(8,128)(2,1)} %copy-done.3, s32[]{:T(128)S(6)} %select_n.4), kind=kLoop, calls=%fused_computation.28 | loop fusion | flops 1835008 | bytes 2752516 | tf_op jit(solution)/shard_map/broadcast_in_dim | solution.py:65
  120.9 2.2 %copy.23 = bf16[1,1792,256]{2,1,0:T(8,128)(2,1)} copy(bf16[1,1792,256]{1,2,0:T(8,128)(2,1)} %fusion.15) | data formatting | bytes 1835008
  123.1 27.4 %collective-permute-done.2 = bf16[1792,256]{1,0:T(8,128)(2,1)} collective-permute-done((bf16[1792,256]{1,0:T(8,128)(2,1)}, bf16[1792,256]{1,0:T(8,128)(2,1)}, u32[]{:S(2)}, u32[]{:S(2)}) %collective-permute-start.2) | collective-permute-done | bytes 917536 | tf_op jit(solution)/shard_map/ppermute | solution.py:44
  150.5 2.6 %fusion.13 = bf16[1,1792,256]{2,1,0:T(8,128)(2,1)} fusion(bf16[1792,256]{1,0:T(8,128)(2,1)} %collective-permute-done.2, bf16[3584,256]{1,0:T(8,128)(2,1)} %convolution_convert_fusion, s32[]{:T(128)S(6)} %select_n.4), kind=kLoop, calls=%fused_computation.26 | loop fusion | flops 1835008 | bytes 2752516 | tf_op jit(solution)/shard_map/broadcast_in_dim | solution.py:65
  153.1 0.0 all-to-all-done
  153.1 1.2 copy.21
  154.3 0.0 copy-done.1
  (16 shorter events, 0.0 us)
Async XLA Ops:
  7.2 1.5 copy-start
  7.2 92.0 %reduce-scatter.2.cloned.1.call-start = ((), (), s32[]{:S(2)}) async-start(), calls=%async_computation.2 | async-start | bytes 8257536 | tf_op jit(solution)/shard_map/reduce_scatter | solution.py:56
  8.7 6.3 %copy-start.2 = (bf16[1,1,64,16,3584]{4,3,2,1,0:T(8,128)(2,1)S(1)}, bf16[1,1,64,16,3584]{4,3,2,1,0:T(8,128)(2,1)}, u32[]{:S(2)}) copy-start(bf16[1,1,64,16,3584]{4,3,2,1,0:T(8,128)(2,1)} %param.7) | copy-start | bytes 22020100
  8.7 6.3 %copy-start.6 = (bf16[1,3584,256]{2,1,0:T(8,128)(2,1)S(1)}, bf16[1,3584,256]{2,1,0:T(8,128)(2,1)}, u32[]{:S(2)}) copy-start(bf16[1,3584,256]{2,1,0:T(8,128)(2,1)} %param.12) | copy-start | bytes 5505028
  15.0 3.1 %copy-start.8 = (f32[1,1,64,16]{2,3,1,0:T(8,128)S(1)}, f32[1,1,64,16]{2,3,1,0:T(8,128)}, u32[]{:S(2)}) copy-start(f32[1,1,64,16]{2,3,1,0:T(8,128)} %param.9) | copy-start | bytes 12292
  15.0 3.1 %copy-start.9 = (s32[1,1,16]{2,1,0:T(1,128)S(1)}, s32[1,1,16]{2,1,0:T(1,128)}, u32[]{:S(2)}) copy-start(s32[1,1,16]{2,1,0:T(1,128)} %param.10) | copy-start | bytes 196
  28.2 7.3 %copy-start.7 = (bf16[1,3584,256]{2,1,0:T(8,128)(2,1)S(1)}, bf16[1,3584,256]{2,1,0:T(8,128)(2,1)}, u32[]{:S(2)}) copy-start(bf16[1,3584,256]{2,1,0:T(8,128)(2,1)} %param.12) | copy-start | bytes 5505028
  51.1 1.6 copy-start.4
  52.7 60.9 %collective-permute-start = (bf16[1792,256]{0,1:T(8,128)(2,1)}, bf16[1792,256]{0,1:T(8,128)(2,1)}, u32[]{:S(2)}, u32[]{:S(2)}) collective-permute-start(bf16[1792,256]{0,1:T(8,128)(2,1)} %dynamic-slice_bitcast_fusion.1), channel_id=1, source_target_pairs={{0,128},{128,0},{1,129},{129,1},{2,130},{130,2},{3,131},{131,3},{4... | collective-permute-start | bytes 2752520 | tf_op jit(solution)/shard_map/ppermute | solution.py:44
  60.4 7.1 %copy-start.3 = (bf16[256,3584]{1,0:T(8,128)(2,1)}, bf16[256,3584]{1,0:T(8,128)(2,1)S(1)}, u32[]{:S(2)}) copy-start(bf16[256,3584]{1,0:T(8,128)(2,1)S(1)} %convolution_convert_fusion.1) | copy-start | bytes 5505028
  61.4 56.7 %collective-permute-start.1 = (bf16[1792,256]{0,1:T(8,128)(2,1)}, bf16[1792,256]{0,1:T(8,128)(2,1)}, u32[]{:S(2)}, u32[]{:S(2)}) collective-permute-start(bf16[1792,256]{0,1:T(8,128)(2,1)} %dynamic-slice_bitcast_fusion), channel_id=1, source_target_pairs={{0,128},{128,0},{1,129},{129,1},{2,130},{130,2},{3,131},{131,3},{4... | collective-permute-start | bytes 2752520 | tf_op jit(solution)/shard_map/ppermute | solution.py:44
  61.8 5.7 %copy-start.10 = (f32[1024,256]{1,0:T(8,128)S(1)}, f32[1024,256]{1,0:T(8,128)}, u32[]{:S(2)}) copy-start(f32[1024,256]{1,0:T(8,128)} %fusion.5) | copy-start | bytes 3145732
  61.8 5.7 %copy-start.11 = (f32[1024,256]{1,0:T(8,128)S(1)}, f32[1024,256]{1,0:T(8,128)}, u32[]{:S(2)}) copy-start(f32[1024,256]{1,0:T(8,128)} %fusion.8) | copy-start | bytes 3145732
  71.3 42.4 %copy-start.5 = (bf16[256,3584]{1,0:T(8,128)(2,1)S(1)}, bf16[256,3584]{1,0:T(8,128)(2,1)}, u32[]{:S(2)}) copy-start(bf16[256,3584]{1,0:T(8,128)(2,1)} %copy-done.4) | copy-start | bytes 5505028
  101.8 51.4 %all-to-all-start = ((bf16[8,16,3584]{2,0,1:T(8,128)(2,1)}), bf16[8,16,3584]{2,0,1:T(8,128)(2,1)S(1)}, u32[]{:S(2)}, u32[]{:S(2)}) async-start(bf16[8,16,3584]{2,0,1:T(8,128)(2,1)} %copy.19), calls=%async_computation.1 | async-start | bytes 1835008 | tf_op jit(solution)/shard_map/all_to_all | solution.py:61
  113.3 37.2 %collective-permute-start.2 = (bf16[1792,256]{1,0:T(8,128)(2,1)}, bf16[1792,256]{1,0:T(8,128)(2,1)}, u32[]{:S(2)}, u32[]{:S(2)}) collective-permute-start(bf16[1792,256]{1,0:T(8,128)(2,1)} %constant_dynamic-slice_fusion), channel_id=1, source_target_pairs={{0,128},{128,0},{1,129},{129,1},{2,130},{130,2},{3,131},{131,3},{4... | collective-permute-start | bytes 2752520 | tf_op jit(solution)/shard_map/ppermute | solution.py:44
  118.2 36.1 %copy-start.1 = (bf16[1,3584,256]{2,1,0:T(8,128)(2,1)S(1)}, bf16[1,3584,256]{2,1,0:T(8,128)(2,1)}, u32[]{:S(2)}) copy-start(bf16[1,3584,256]{2,1,0:T(8,128)(2,1)} %param.11) | copy-start | bytes 5505028
Sparse Core Ops, SparseCore 0:
  45.9 53.2 reduce-scatter.1

commit v2 on v0

v2 whole, which is shorter than its diff:
```python
import functools

import jax
import jax.numpy as jnp
from jax import lax
from jax.experimental import pallas as pl
from jax.experimental.pallas import tpu as pltpu
from jax.sharding import PartitionSpec as P

RING = 4
BF16 = jnp.bfloat16
F32 = jnp.float32


def dot_nt(a, b):
    return lax.dot_general(a, b, (((1,), (1,)), ((), ())), preferred_element_type=F32)


def dot_tn(a, b):
    return lax.dot_general(a, b, (((0,), (0,)), ((), ())), preferred_element_type=F32)


def swap_matrix(size, inner_in, inner_out):
    row = lax.broadcasted_iota(jnp.int32, (size, size), 0)
    col = lax.broadcasted_iota(jnp.int32, (size, size), 1)
    source = (row % inner_out) * inner_in + row // inner_out
    return (col == source).astype(BF16)


def layer_kernel(
    nodes, chunk, tile,
    tok_hbm, grd_hbm, scale_ref, wg_hbm, wu_hbm, wd_hbm,
    dtok_out, gate_out, up_out, down_out,
    tok, scl, wg, wu, wd, hid, act, actp, tok_o, act_o,
    msend, mrecv, csum, orecv, nrecv, afin, arecv, dfin, dsend, drecv, wfin,
    load_sem, tz_sem, az_sem, m_sem, ag_sem, fw_sem, o_sem, n_sem, a_sem, dz_sem, out_sem,
):
    rows, width = tok.shape
    hl = wg.shape[1]
    half = width // 2
    group = rows // (2 * RING)
    block = rows // RING
    slots = group // nodes
    steps = width // chunk
    side = chunk // 2
    tiles = half // tile

    mine = lax.axis_index("dp")
    node = lax.axis_index("node")
    local = lax.axis_index("local")
    core = lax.rem(local, 2)
    place = lax.div(local, 2)
    other = 1 - mine
    mate = local + 1 - 2 * core

    def at_place(step):
        return lax.rem(place + step, RING)

    def peer(step):
        return at_place(step) * 2 + core

    def load(src, dst, index):
        return pltpu.make_async_copy(src, dst, load_sem.at[index])

    def block_rows(b):
        return pl.ds(pl.multiple_of(b * block, block), block)

    def tok_load(b):
        return load(tok_hbm.at[block_rows(b)], tok.at[block_rows(b)], 3 + b)

    def grd_load(b):
        return load(grd_hbm.at[block_rows(b)], scl.at[block_rows(b)], 3 + RING + b)

    load_wg = load(wg_hbm, wg, 0)
    load_wu = load(wu_hbm, wu, 1)
    load_wd = load(wd_hbm, wd, 2)
    load_wg.start()
    tok_load(0).start()
    load_wu.start()
    load_wd.start()
    grd_load(0).start()
    for b in range(1, RING):
        tok_load(b).start()
        grd_load(b).start()

    barrier = pltpu.get_barrier_semaphore()
    pl.semaphore_signal(barrier, inc=1, device_id={"dp": other})
    pl.semaphore_signal(barrier, inc=1, device_id={"local": mate})
    for step in range(1, RING):
        pl.semaphore_signal(barrier, inc=1, device_id={"local": peer(step)})

    def greet(i, carry):
        pl.semaphore_signal(barrier, inc=1, device_id={"node": lax.rem(node + i, nodes)})
        return carry

    lax.fori_loop(1, nodes, greet, 0)
    pl.semaphore_wait(barrier, 2 + RING - 1 + nodes - 1)

    def group_rows(l):
        return pl.ds(pl.multiple_of(l * group, group), group)

    tz = pltpu.make_async_remote_copy(
        tok_hbm.at[group_rows(local), pl.ds(pl.multiple_of(other * half, 128), half)],
        tok_o.at[group_rows(local)],
        tz_sem.at[0], tz_sem.at[1], device_id={"dp": other},
    )
    tz.start()

    def az(b):
        return pltpu.make_async_remote_copy(
            act.at[block_rows(b)], act_o.at[block_rows(b)],
            az_sem.at[0, b], az_sem.at[1, b], device_id={"dp": other},
        )

    swap_in = swap_matrix(group, nodes, slots)
    load_wg.wait()
    load_wu.wait()
    load_wd.wait()

    def forward(b, carry):
        here = block_rows(b)
        tok_load(b).wait()
        rows_in = tok[here, :]
        gate = jnp.dot(rows_in, wg[...], preferred_element_type=F32)
        up = jnp.dot(rows_in, wu[...], preferred_element_type=F32)
        grd_load(b).wait()
        scaled = (scl[here, :].astype(F32) * scale_ref[here, :]).astype(BF16)
        scl[here, :] = scaled
        back = jnp.dot(scaled, wd[...], preferred_element_type=F32)
        sig = jax.nn.sigmoid(gate)
        silu = gate * sig
        hid[here, :] = (silu * up).astype(BF16)
        gate_grad = (back * up * sig * (1.0 + gate * (1.0 - sig))).astype(BF16)
        up_grad = (back * silu).astype(BF16)
        act[here, :hl] = gate_grad
        act[here, hl:] = up_grad
        az(b).start()
        for i in range(2):
            part = slice(i * group, (i + 1) * group)
            there = pl.ds(pl.multiple_of((i * RING + b) * group, group), group)
            actp[there, :hl] = jnp.dot(
                swap_in, gate_grad[part], preferred_element_type=F32
            ).astype(BF16)
            actp[there, hl:] = jnp.dot(
                swap_in, up_grad[part], preferred_element_type=F32
            ).astype(BF16)
        return carry

    lax.fori_loop(0, RING, forward, 0)

    def partial(which, q):
        cols = pl.ds(pl.multiple_of(q * chunk, chunk), chunk)
        here = pl.ds(pl.multiple_of(which * (rows // 2), rows // 2), rows // 2)
        return dot_nt(actp[here, :hl], wg[cols, :]) + dot_nt(actp[here, hl:], wu[cols, :])

    def to_mate(q):
        return pltpu.make_async_remote_copy(
            msend.at[q], mrecv.at[q], m_sem.at[0, q], m_sem.at[1, q], device_id={"local": mate}
        )

    def give(q, carry):
        msend[q] = partial(1 - core, q).astype(BF16)
        to_mate(q).start()
        return carry

    lax.fori_loop(0, steps, give, 0)

    def spread(step):
        return pltpu.make_async_remote_copy(
            tok_o.at[group_rows(local)], tok_o.at[group_rows(local)],
            ag_sem.at[0, step], ag_sem.at[1, step], device_id={"local": peer(step)},
        )

    def hand_on(step):
        rows_of = group_rows(peer(step))
        return pltpu.make_async_remote_copy(
            tok_o.at[rows_of], tok_o.at[rows_of],
            fw_sem.at[0, step], fw_sem.at[1, step], device_id={"local": mate},
        )

    tz.wait_recv()
    for step in range(1, RING):
        spread(step).start()
    hand_on(0).start()

    def part_rows(step):
        return pl.ds(pl.multiple_of(at_place(step) * group, group), group)

    def opposite(q, way):
        return pltpu.make_async_remote_copy(
            csum.at[q, part_rows(2), pl.ds(way * side, side)],
            orecv.at[q, way],
            o_sem.at[0, q, way], o_sem.at[1, q, way],
            device_id={"local": peer(1 if way == 0 else RING - 1)},
        )

    def neighbour(q, way):
        step = 1 if way == 0 else RING - 1
        return pltpu.make_async_remote_copy(
            csum.at[q, part_rows(step)],
            nrecv.at[q, way],
            n_sem.at[0, q, way], n_sem.at[1, q, way],
            device_id={"local": peer(step)},
        )

    def to_nodes(q):
        return pltpu.make_async_remote_copy(
            afin.at[q, pl.ds(0, nodes - 1)], arecv.at[q, pl.ds(0, nodes - 1)],
            a_sem.at[0, q], a_sem.at[1, q], device_id={"node": lax.rem(node + 1, nodes)},
        )

    def chip_sum(q):
        to_mate(q).wait_recv()
        total = partial(core, q) + mrecv[q].astype(F32)
        csum[q] = total.astype(BF16)
        opposite(q, 0).start()
        opposite(q, 1).start()

    def pass_on(q):
        for way in range(2):
            opposite(q, way).wait_recv()
            here = part_rows(1 if way == 0 else RING - 1)
            cols = slice(way * side, (way + 1) * side)
            csum[q, here, cols] = (
                csum[q, here, cols].astype(F32) + orecv[q, way].astype(F32)
            ).astype(BF16)
            neighbour(q, way).start()

    def finish(q):
        neighbour(q, 0).wait_recv()
        neighbour(q, 1).wait_recv()
        total = csum[q, part_rows(0)].astype(F32) + nrecv[q, 0].astype(F32) + nrecv[q, 1].astype(F32)
        afin[q] = total.reshape(nodes, slots, chunk).astype(BF16)
        arecv[q, node] = afin[q, node]

        def send(i, carry):
            to = lax.rem(node + i, nodes)
            pltpu.make_async_remote_copy(
                afin.at[q, to], arecv.at[q, node],
                a_sem.at[0, q], a_sem.at[1, q], device_id={"node": to},
            ).start()
            return carry

        lax.fori_loop(1, nodes, send, 0)

    def tile_cols(which, k):
        return pl.ds(pl.multiple_of(which * half + k * tile, 128), tile)

    def tile_rows(k):
        return pl.ds(pl.multiple_of(k * tile, tile), tile)

    def dz(k):
        return pltpu.make_async_remote_copy(
            dsend.at[tile_rows(k)], drecv.at[tile_rows(k)],
            dz_sem.at[0, k], dz_sem.at[1, k], device_id={"dp": other},
        )

    def down_other(k, carry):
        dsend[tile_rows(k), :] = dot_tn(scl[:, tile_cols(other, k)], hid[...]).astype(BF16)
        dz(k).start()
        return carry

    chip_sum(0)
    chip_sum(1)
    lax.fori_loop(0, tiles, down_other, 0)

    def pipeline(s, carry):
        @pl.when(s < steps)
        def _():
            chip_sum(s)

        @pl.when(jnp.logical_and(s >= 1, s < steps + 1))
        def _():
            pass_on(s - 1)

        @pl.when(s >= 3)
        def _():
            finish(s - 3)

        return carry

    pass_on(0)
    lax.fori_loop(2, steps + 3, pipeline, 0)

    for step in range(1, RING):
        pltpu.make_async_remote_copy(
            tok_o.at[group_rows(peer(RING - step))], tok_o.at[group_rows(peer(RING - step))],
            ag_sem.at[0, step], ag_sem.at[1, step], device_id={"local": peer(step)},
        ).wait_recv()
        hand_on(RING - step).start()
    for step in range(RING):
        hand_on(step).wait_recv()
    for b in range(RING):
        az(b).wait_recv()

    def put(which, k, out):
        return pltpu.make_async_copy(
            wfin.at[which, tile_rows(k)], out.at[tile_rows(k)], out_sem.at[which, k]
        )

    def weights(k, carry):
        here = tile_rows(k)
        dz(k).wait_recv()
        down = dot_tn(scl[:, tile_cols(mine, k)], hid[...]).astype(BF16).astype(F32)
        wfin[2, here, :] = (down + drecv[here, :].astype(F32)).astype(BF16)
        put(2, k, down_out).start()
        both = dot_tn(tok[:, tile_cols(mine, k)], act[...]) + dot_tn(
            tok_o[:, tile_cols(0, k)], act_o[...]
        )
        wfin[0, here, :] = both[:, :hl].astype(BF16)
        wfin[1, here, :] = both[:, hl:].astype(BF16)
        put(0, k, gate_out).start()
        put(1, k, up_out).start()
        return carry

    lax.fori_loop(0, tiles, weights, 0)

    swap_out = swap_matrix(group, slots, nodes)

    def put_rows(q):
        cols = pl.ds(pl.multiple_of(q * chunk, chunk), chunk)
        return pltpu.make_async_copy(dfin.at[q], dtok_out.at[:, cols], out_sem.at[3, q])

    def collect(q, carry):
        to_nodes(q).wait_recv()
        got = arecv[q].astype(F32).reshape(group, chunk).astype(BF16)
        dfin[q] = jnp.dot(swap_out, got, preferred_element_type=F32).astype(BF16)
        put_rows(q).start()
        return carry

    lax.fori_loop(0, steps, collect, 0)

    tz.wait_send()
    for b in range(RING):
        az(b).wait_send()
    for step in range(1, RING):
        spread(step).wait_send()
    for step in range(RING):
        hand_on(step).wait_send()

    def drain(q, carry):
        to_mate(q).wait_send()
        for way in range(2):
            opposite(q, way).wait_send()
            neighbour(q, way).wait_send()
        to_nodes(q).wait_send()
        put_rows(q).wait()
        return carry

    lax.fori_loop(0, steps, drain, 0)

    def drain_weights(k, carry):
        dz(k).wait_send()
        put(0, k, gate_out).wait()
        put(1, k, up_out).wait()
        put(2, k, down_out).wait()
        return carry

    lax.fori_loop(0, tiles, drain_weights, 0)


def on_device(chunk, tile, tokens_in, grad_rows, combine_weights, live_counts, w_gate, w_up, w_down):
    slot_count, nodes, width = tokens_in.shape[2:]
    rows = slot_count * nodes
    hl = w_gate.shape[2]
    half = width // 2
    group = rows // (2 * RING)
    steps = width // chunk
    tiles = half // tile
    live_mask = (
        lax.broadcasted_iota(jnp.int32, (slot_count, nodes), 0) < live_counts[0, 0][None, :]
    ).astype(F32)
    scale = (combine_weights[0, 0] * live_mask).reshape(rows, 1)
    anywhere = pl.BlockSpec(memory_space=pl.ANY)
    dma = pltpu.SemaphoreType.DMA
    vmem = pltpu.VMEM
    weight_shape = jax.ShapeDtypeStruct((half, hl), BF16)
    d_tokens, gate, up, down = pl.pallas_call(
        functools.partial(layer_kernel, nodes, chunk, tile),
        out_shape=(jax.ShapeDtypeStruct((group, width), BF16), weight_shape, weight_shape, weight_shape),
        in_specs=[anywhere, anywhere, pl.BlockSpec(memory_space=vmem), anywhere, anywhere, anywhere],
        out_specs=(anywhere, anywhere, anywhere, anywhere),
        scratch_shapes=[
            vmem((rows, width), BF16),
            vmem((rows, width), BF16),
            vmem((width, hl), BF16),
            vmem((width, hl), BF16),
            vmem((width, hl), BF16),
            vmem((rows, hl), BF16),
            vmem((rows, 2 * hl), BF16),
            vmem((rows, 2 * hl), BF16),
            vmem((rows, half), BF16),
            vmem((rows, 2 * hl), BF16),
            vmem((steps, rows // 2, chunk), BF16),
            vmem((steps, rows // 2, chunk), BF16),
            vmem((steps, rows // 2, chunk), BF16),
            vmem((steps, 2, group, chunk // 2), BF16),
            vmem((steps, 2, group, chunk), BF16),
            vmem((steps, nodes, group // nodes, chunk), BF16),
            vmem((steps, nodes, group // nodes, chunk), BF16),
            vmem((steps, group, chunk), BF16),
            vmem((half, hl), BF16),
            vmem((half, hl), BF16),
            vmem((3, half, hl), BF16),
            dma((3 + 2 * RING,)),
            dma((2,)),
            dma((2, RING)),
            dma((2, steps)),
            dma((2, RING)),
            dma((2, RING)),
            dma((2, steps, 2)),
            dma((2, steps, 2)),
            dma((2, steps)),
            dma((2, tiles)),
            dma((4, max(tiles, steps))),
        ],
        compiler_params=pltpu.CompilerParams(
            collective_id=0, has_side_effects=True, vmem_limit_bytes=VMEM_LIMIT
        ),
        name="expert_backward",
    )(
        tokens_in[0, 0].reshape(rows, width),
        grad_rows[0, 0].reshape(rows, width),
        scale,
        w_gate[0],
        w_up[0],
        w_down[0],
    )
    return (
        d_tokens.reshape(1, 1, group // nodes, nodes, width),
        gate[None],
        up[None],
        down[None],
    )


VMEM_LIMIT = 62 * 1024 * 1024
CHUNK = 512
TILE = 256


def solution(mesh):
    return jax.shard_map(
        functools.partial(on_device, CHUNK, TILE),
        mesh=mesh,
        in_specs=(
            P("dp", "node", None, None, None),
            P("dp", "node", None, None, None),
            P("dp", "node", None, None),
            P("dp", "node", None),
            P("node", None, "local"),
            P("node", None, "local"),
            P("node", None, "local"),
        ),
        out_specs=(
            P("dp", "node", "local", None, None),
            P("node", "dp", "local"),
            P("node", "dp", "local"),
            P("node", "dp", "local"),
        ),
        check_vma=False,
    )
```

time: 214 us -> 101 us (0.47)
  waiting for transfers between devices: 115 us -> 0 us
  Pallas kernels: 0 us -> 92.5 us
  matrix products: 40.2 us -> 0 us
  local copies, waits for them, and re-layouts: 20.2 us -> 6.47 us
  between operations: 14.1 us -> 0.68 us
  other arithmetic: 13.9 us -> 1.52 us
  starting transfers between devices: 9.47 us -> 0 us
    pallas_call x0 -> x1, Pallas kernels: none -> 92.5 us  [on_device(): pl.pallas_call(functools.partial(layer_kernel, nodes, chunk, tile), out_s...]
    reduce_scatter x1 -> x0, waiting for transfers between devices: 81.9 us -> none  [on_device(): lax.psum_scatter(jnp.concatenate((front, behind), axis=1).astype(jnp.bflo...]
    dot_general x7 -> x0, matrix products: 40.2 us -> none  [the longest x1 7.78 us: on_device(): lax.dot_general(flat_tokens, joined_grad, (((0,), (0,)), ((), ())), prefe...]
    unnamed x3 -> x0, waiting for transfers between devices: 33.2 us -> none
    convert_element_type x2 -> x0, other arithmetic: 11.1 us -> none  [on_device(): scaled_rows = (grad_rows[0, 0].astype(jnp.float32) * (combine_weights[0,...]
    unnamed x20 -> x11, local copies, waits for them, and re-layouts: 16.5 us -> 5.85 us
    all_to_all x1 -> x0, starting transfers between devices: 9.39 us -> none  [on_device(): lax.all_to_all(summed, 'node', split_axis=1, concat_axis=1, tiled=True)]
    broadcast_in_dim x1 -> x0, local copies, waits for them, and re-layouts: 3.32 us -> none  [on_device(): grad_down = weight_sums[:, 2 * hid_local:].astype(jnp.bfloat16)[None]]
  transfers between devices with their start and end apart: 3 -> 0, of which waited for: 2 -> 0; matrix products, arithmetic and copies ran while one was open for 14% -> 0% of each run, Pallas kernels for 0% -> 0%
where the time goes in v2:
time: 101 us
  Pallas kernels  92.5 us (92%)
  local copies, waits for them, and re-layouts  6.47 us (6%)
  other arithmetic  1.52 us (2%)
    pallas_call x1, Pallas kernels, on_device(): pl.pallas_call(functools.partial(layer_kernel, nodes, chunk, tile), out_s...  92.5 us
    unnamed x11, local copies, waits for them, and re-layouts  5.85 us

profile of v2, /device:TPU:1, one launch (start us, length us, event | category | flops | bytes accessed | tf_op | source)
XLA Modules:
  0.0 101.1 jit_solution(14645387313225867368)
XLA Ops:
  0.6 0.7 iota_compare_fusion
  1.3 0.8 copy.12
  2.1 0.3 lt.24
  2.4 0.3 squeeze.16
  2.7 0.8 broadcast_select_fusion.scale_ref
  3.6 92.5 %expert_backward.1 = (bf16[128,3584]{1,0:T(8,128)(2,1)}, bf16[1792,256]{1,0:T(8,128)(2,1)}, bf16[1792,256]{1,0:T(8,128)(2,1)}, bf16[1792,256]{1,0:T(8,128)(2,1)}) custom-call(bf16[1024,3584]{1,0:T(8,128)(2,1)} %bitcast.12, bf16[1024,3584]{1,0:T(8,128)(2,1)} %bitcast.13, f32[1024,1]{1,0:T(8,128)} %broadcast_select_fusion.scale_ref, ...), custom_call_target="tpu_custom_call" | custom-call | tf_op jit(solution)/shard_map/expert_backward/pallas_call | solution.py:378
  96.0 0.0 copy-start.2
  96.1 0.0 copy-start.1
  96.1 2.3 %copy.19 = bf16[1,1,8,16,3584]{4,3,2,1,0:T(8,128)(2,1)} copy(bf16[1,1,8,16,3584]{4,3,2,1,0:T(8,128)(2,1)} %bitcast.20) | data formatting | bytes 1835008
  98.4 0.0 copy-done.2
  98.4 0.0 copy-start
  98.4 0.9 copy.20
  99.3 0.0 copy-done.1
  99.3 0.9 copy.21
  100.2 0.0 copy-done
  100.2 0.9 copy.22
Async XLA Ops:
  96.0 2.3 %copy-start.2 = (bf16[1792,256]{1,0:T(8,128)(2,1)S(1)}, bf16[1792,256]{1,0:T(8,128)(2,1)}, u32[]{:S(2)}) copy-start(bf16[1792,256]{1,0:T(8,128)(2,1)} %get-tuple-element.9) | copy-start | bytes 2752516
  96.1 3.2 %copy-start.1 = (bf16[1792,256]{1,0:T(8,128)(2,1)S(1)}, bf16[1792,256]{1,0:T(8,128)(2,1)}, u32[]{:S(2)}) copy-start(bf16[1792,256]{1,0:T(8,128)(2,1)} %get-tuple-element.10) | copy-start | bytes 2752516
  98.4 1.9 %copy-start = (bf16[1792,256]{1,0:T(8,128)(2,1)S(1)}, bf16[1792,256]{1,0:T(8,128)(2,1)}, u32[]{:S(2)}) copy-start(bf16[1792,256]{1,0:T(8,128)(2,1)} %get-tuple-element.11) | copy-start | bytes 2752516

commit v3 on v2

--- a/solution.py
+++ b/solution.py
@@ -29,7 +29,7 @@
 
 def layer_kernel(
     nodes, chunk, tile,
-    tok_hbm, grd_hbm, scale_ref, wg_hbm, wu_hbm, wd_hbm,
+    tok_hbm, grd_hbm, weight_ref, count_ref, wg_hbm, wu_hbm, wd_hbm,
     dtok_out, gate_out, up_out, down_out,
     tok, scl, wg, wu, wd, hid, act, actp, tok_o, act_o,
     msend, mrecv, csum, orecv, nrecv, afin, arecv, dfin, dsend, drecv, wfin,
@@ -41,6 +41,7 @@
     group = rows // (2 * RING)
     block = rows // RING
     slots = group // nodes
+    piece = group // RING
     steps = width // chunk
     side = chunk // 2
     tiles = half // tile
@@ -75,13 +76,10 @@
     load_wu = load(wu_hbm, wu, 1)
     load_wd = load(wd_hbm, wd, 2)
     load_wg.start()
+    load_wu.start()
     tok_load(0).start()
-    load_wu.start()
     load_wd.start()
     grd_load(0).start()
-    for b in range(1, RING):
-        tok_load(b).start()
-        grd_load(b).start()
 
     barrier = pltpu.get_barrier_semaphore()
     pl.semaphore_signal(barrier, inc=1, device_id={"dp": other})
@@ -99,12 +97,31 @@
     def group_rows(l):
         return pl.ds(pl.multiple_of(l * group, group), group)
 
-    tz = pltpu.make_async_remote_copy(
-        tok_hbm.at[group_rows(local), pl.ds(pl.multiple_of(other * half, 128), half)],
-        tok_o.at[group_rows(local)],
-        tz_sem.at[0], tz_sem.at[1], device_id={"dp": other},
-    )
-    tz.start()
+    def piece_rows(l, p):
+        return pl.ds(pl.multiple_of(l * group + p * piece, piece), piece)
+
+    def tz(p):
+        return pltpu.make_async_remote_copy(
+            tok_hbm.at[piece_rows(local, p), pl.ds(pl.multiple_of(other * half, 128), half)],
+            tok_o.at[piece_rows(local, p)],
+            tz_sem.at[0, p], tz_sem.at[1, p], device_id={"dp": other},
+        )
+
+    for p in range(RING):
+        tz(p).start()
+    tok_load(1).start()
+    grd_load(1).start()
+
+    def spread(step, p):
+        return pltpu.make_async_remote_copy(
+            tok_o.at[piece_rows(local, p)], tok_o.at[piece_rows(local, p)],
+            ag_sem.at[0, step, p], ag_sem.at[1, step, p], device_id={"local": peer(step)},
+        )
+
+    def spread_piece(p):
+        tz(p).wait_recv()
+        for step in range(1, RING):
+            spread(step, p).start()
 
     def az(b):
         return pltpu.make_async_remote_copy(
@@ -113,18 +130,44 @@
         )
 
     swap_in = swap_matrix(group, nodes, slots)
+
+    eye = lax.broadcasted_iota(jnp.int32, (nodes, nodes), 0) == lax.broadcasted_iota(
+        jnp.int32, (nodes, nodes), 1
+    )
+    counts = jnp.broadcast_to(count_ref[...].astype(F32), (nodes, nodes))
+    counts = jnp.sum(jnp.where(eye, counts, 0.0), axis=1, keepdims=True)
+    slot_total = weight_ref.shape[1]
+    slot_at = lax.broadcasted_iota(jnp.int32, (nodes, slot_total), 1).astype(F32)
+    live_weights = jnp.where(slot_at < counts, weight_ref[...], 0.0)
+    row_weights = jnp.tile(live_weights, (block // nodes, 1))
+    row_slot = lax.broadcasted_iota(jnp.int32, (block, slot_total), 0) // nodes
+    slot_lane = lax.broadcasted_iota(jnp.int32, (block, slot_total), 1)
+
     load_wg.wait()
     load_wu.wait()
-    load_wd.wait()
 
     def forward(b, carry):
         here = block_rows(b)
         tok_load(b).wait()
+        grd_load(b).wait()
+
+        @pl.when(b == 0)
+        def _():
+            load_wd.wait()
+
+        @pl.when(b < RING - 2)
+        def _():
+            tok_load(b + 2).start()
+            grd_load(b + 2).start()
+
+        scale = jnp.sum(
+            jnp.where(slot_lane == row_slot + b * (block // nodes), row_weights, 0.0),
+            axis=1, keepdims=True,
+        )
         rows_in = tok[here, :]
         gate = jnp.dot(rows_in, wg[...], preferred_element_type=F32)
         up = jnp.dot(rows_in, wu[...], preferred_element_type=F32)
-        grd_load(b).wait()
-        scaled = (scl[here, :].astype(F32) * scale_ref[here, :]).astype(BF16)
+        scaled = (scl[here, :].astype(F32) * scale).astype(BF16)
         scl[here, :] = scaled
         back = jnp.dot(scaled, wd[...], preferred_element_type=F32)
         sig = jax.nn.sigmoid(gate)
@@ -144,6 +187,11 @@
             actp[there, hl:] = jnp.dot(
                 swap_in, up_grad[part], preferred_element_type=F32
             ).astype(BF16)
+
+        @pl.when(b >= 1)
+        def _():
+            spread_piece(b - 1)
+
         return carry
 
     lax.fori_loop(0, RING, forward, 0)
@@ -158,18 +206,9 @@
             msend.at[q], mrecv.at[q], m_sem.at[0, q], m_sem.at[1, q], device_id={"local": mate}
         )
 
-    def give(q, carry):
+    def give(q):
         msend[q] = partial(1 - core, q).astype(BF16)
         to_mate(q).start()
-        return carry
-
-    lax.fori_loop(0, steps, give, 0)
-
-    def spread(step):
-        return pltpu.make_async_remote_copy(
-            tok_o.at[group_rows(local)], tok_o.at[group_rows(local)],
-            ag_sem.at[0, step], ag_sem.at[1, step], device_id={"local": peer(step)},
-        )
 
     def hand_on(step):
         rows_of = group_rows(peer(step))
@@ -177,11 +216,6 @@
             tok_o.at[rows_of], tok_o.at[rows_of],
             fw_sem.at[0, step], fw_sem.at[1, step], device_id={"local": mate},
         )
-
-    tz.wait_recv()
-    for step in range(1, RING):
-        spread(step).start()
-    hand_on(0).start()
 
     def part_rows(step):
         return pl.ds(pl.multiple_of(at_place(step) * group, group), group)
@@ -255,39 +289,57 @@
             dz_sem.at[0, k], dz_sem.at[1, k], device_id={"dp": other},
         )
 
-    def down_other(k, carry):
+    def down_other(k):
         dsend[tile_rows(k), :] = dot_tn(scl[:, tile_cols(other, k)], hid[...]).astype(BF16)
         dz(k).start()
-        return carry
-
-    chip_sum(0)
-    chip_sum(1)
-    lax.fori_loop(0, tiles, down_other, 0)
 
     def pipeline(s, carry):
         @pl.when(s < steps)
         def _():
-            chip_sum(s)
-
-        @pl.when(jnp.logical_and(s >= 1, s < steps + 1))
-        def _():
-            pass_on(s - 1)
-
-        @pl.when(s >= 3)
-        def _():
-            finish(s - 3)
-
-        return carry
-
-    pass_on(0)
-    lax.fori_loop(2, steps + 3, pipeline, 0)
-
-    for step in range(1, RING):
-        pltpu.make_async_remote_copy(
-            tok_o.at[group_rows(peer(RING - step))], tok_o.at[group_rows(peer(RING - step))],
-            ag_sem.at[0, step], ag_sem.at[1, step], device_id={"local": peer(step)},
-        ).wait_recv()
-        hand_on(RING - step).start()
+            give(s)
+
+        @pl.when(s == 1)
+        def _():
+            spread_piece(RING - 1)
+            hand_on(0).start()
+
+        @pl.when(jnp.logical_and(s >= 2, s < steps + 2))
+        def _():
+            chip_sum(s - 2)
+
+        for i in range(2):
+            k = (s - 2) * 2 + i
+
+            @pl.when(jnp.logical_and(k >= 0, k < tiles))
+            def _():
+                down_other(k)
+
+        @pl.when(jnp.logical_and(s >= 4, s < steps + 4))
+        def _():
+            pass_on(s - 4)
+
+        @pl.when(s == 6)
+        def _():
+            hand_on_arrivals()
+
+        @pl.when(s >= 6)
+        def _():
+            finish(s - 6)
+
+        return carry
+
+    def hand_on_arrivals():
+        for step in range(1, RING):
+            for p in range(RING):
+                rows_of = piece_rows(peer(RING - step), p)
+                pltpu.make_async_remote_copy(
+                    tok_o.at[rows_of], tok_o.at[rows_of],
+                    ag_sem.at[0, step, p], ag_sem.at[1, step, p], device_id={"local": peer(step)},
+                ).wait_recv()
+            hand_on(RING - step).start()
+
+    lax.fori_loop(0, steps + 6, pipeline, 0)
+
     for step in range(RING):
         hand_on(step).wait_recv()
     for b in range(RING):
@@ -330,11 +382,12 @@
 
     lax.fori_loop(0, steps, collect, 0)
 
-    tz.wait_send()
     for b in range(RING):
+        tz(b).wait_send()
         az(b).wait_send()
     for step in range(1, RING):
-        spread(step).wait_send()
+        for p in range(RING):
+            spread(step, p).wait_send()
     for step in range(RING):
         hand_on(step).wait_send()
 
@@ -357,6 +410,21 @@
         return carry
 
     lax.fori_loop(0, tiles, drain_weights, 0)
+
+
+def copy_kernel(count, *refs):
+    sems = refs[2 * count]
+    copies = []
+    for i in range(count):
+        src, dst = refs[i], refs[count + i]
+        part = src.shape[0] // 2
+        for h in range(2):
+            span = pl.ds(h * part, part)
+            copies.append(pltpu.make_async_copy(src.at[span], dst.at[span], sems.at[2 * i + h]))
+    for copy in copies:
+        copy.start()
+    for copy in copies:
+        copy.wait()
 
 
 def on_device(chunk, tile, tokens_in, grad_rows, combine_weights, live_counts, w_gate, w_up, w_down):
@@ -367,18 +435,15 @@
     group = rows // (2 * RING)
     steps = width // chunk
     tiles = half // tile
-    live_mask = (
-        lax.broadcasted_iota(jnp.int32, (slot_count, nodes), 0) < live_counts[0, 0][None, :]
-    ).astype(F32)
-    scale = (combine_weights[0, 0] * live_mask).reshape(rows, 1)
     anywhere = pl.BlockSpec(memory_space=pl.ANY)
     dma = pltpu.SemaphoreType.DMA
     vmem = pltpu.VMEM
     weight_shape = jax.ShapeDtypeStruct((half, hl), BF16)
-    d_tokens, gate, up, down = pl.pallas_call(
+    held = pl.pallas_call(
         functools.partial(layer_kernel, nodes, chunk, tile),
         out_shape=(jax.ShapeDtypeStruct((group, width), BF16), weight_shape, weight_shape, weight_shape),
-        in_specs=[anywhere, anywhere, pl.BlockSpec(memory_space=vmem), anywhere, anywhere, anywhere],
+        in_specs=[anywhere, anywhere, pl.BlockSpec(memory_space=vmem),
+                  pl.BlockSpec(memory_space=vmem), anywhere, anywhere, anywhere],
         out_specs=(anywhere, anywhere, anywhere, anywhere),
         scratch_shapes=[
             vmem((rows, width), BF16),
@@ -403,10 +468,10 @@
             vmem((half, hl), BF16),
             vmem((3, half, hl), BF16),
             dma((3 + 2 * RING,)),
-            dma((2,)),
+            dma((2, RING)),
             dma((2, RING)),
             dma((2, steps)),
-            dma((2, RING)),
+            dma((2, RING, RING)),
             dma((2, RING)),
             dma((2, steps, 2)),
             dma((2, steps, 2)),
@@ -421,11 +486,20 @@
     )(
         tokens_in[0, 0].reshape(rows, width),
         grad_rows[0, 0].reshape(rows, width),
-        scale,
+        combine_weights[0, 0].T,
+        live_counts[0],
         w_gate[0],
         w_up[0],
         w_down[0],
     )
+    d_tokens, gate, up, down = pl.pallas_call(
+        functools.partial(copy_kernel, len(held)),
+        out_shape=tuple(jax.ShapeDtypeStruct(a.shape, a.dtype) for a in held),
+        in_specs=[anywhere] * len(held),
+        out_specs=tuple([anywhere] * len(held)),
+        scratch_shapes=[dma((2 * len(held),))],
+        name="write_out",
+    )(*held)
     return (
         d_tokens.reshape(1, 1, group // nodes, nodes, width),
         gate[None],

time: 101 us -> 200 us (1.98)
  Pallas kernels: 92.5 us -> 198 us
  local copies, waits for them, and re-layouts: 6.47 us -> 0 us
    pallas_call x0 -> x1, Pallas kernels: none -> 112 us  [on_device(): pl.pallas_call(functools.partial(copy_kernel, len(held)), out_shape=tuple...]
    pallas_call x1, Pallas kernels: 92.5 us -> 85.6 us  [on_device(): pl.pallas_call(functools.partial(layer_kernel, nodes, chunk, tile), out_s...]
    unnamed x11 -> x0, local copies, waits for them, and re-layouts: 5.85 us -> none
where the time goes in v3:
time: 200 us; the launch traced here: 199 us
  Pallas kernels  198 us (99%)
    pallas_call x1, Pallas kernels, on_device(): pl.pallas_call(functools.partial(copy_kernel, len(held)), out_shape=tuple...  112 us
    pallas_call x1, Pallas kernels, on_device(): pl.pallas_call(functools.partial(layer_kernel, nodes, chunk, tile), out_s...  85.6 us

profile of v3, /device:TPU:1, one launch (start us, length us, event | category | flops | bytes accessed | tf_op | source)
XLA Modules:
  0.0 198.6 jit_solution(13272016653127918519)
XLA Ops:
  0.6 85.6 %expert_backward.1 = (bf16[128,3584]{1,0:T(8,128)(2,1)}, bf16[1792,256]{1,0:T(8,128)(2,1)}, bf16[1792,256]{1,0:T(8,128)(2,1)}, bf16[1792,256]{1,0:T(8,128)(2,1)}) custom-call(bf16[1024,3584]{1,0:T(8,128)(2,1)} %bitcast.13, bf16[1024,3584]{1,0:T(8,128)(2,1)} %bitcast.14, f32[16,64]{1,0:T(8,128)} %bitcast.18, s32[1,16]{1,0:T(1,128)} %bitcast.19, ...), custom_call_target="tpu_custom_call" | custom-call | tf_op jit(solution)/shard_map/expert_backward/pallas_call | solution.py:442
  86.3 112.4 %write_out.1 = (bf16[128,3584]{1,0:T(8,128)(2,1)}, bf16[1792,256]{1,0:T(8,128)(2,1)}, bf16[1792,256]{1,0:T(8,128)(2,1)}, bf16[1792,256]{1,0:T(8,128)(2,1)}) custom-call(bf16[128,3584]{1,0:T(8,128)(2,1)} %get-tuple-element.12.refs_0_, bf16[1792,256]{1,0:T(8,128)(2,1)} %get-tuple-element.13.refs_1_, bf16[1792,256]{1,0:T(8,128)(2,1)} %get-tuple-element.14.refs_2_, ...), custom_call_target="tpu_custom_call" | custom-call | tf_op jit(solution)/shard_map/write_out/pallas_call | solution.py:495

commit v4 on v3

--- a/solution.py
+++ b/solution.py
@@ -413,18 +413,26 @@
 
 
 def copy_kernel(count, *refs):
-    sems = refs[2 * count]
-    copies = []
+    sources, results, held = refs[:count], refs[count : 2 * count], refs[2 * count : 3 * count]
+    sems = refs[3 * count]
+    reads, writes = [], []
     for i in range(count):
-        src, dst = refs[i], refs[count + i]
-        part = src.shape[0] // 2
+        part = sources[i].shape[0] // 2
         for h in range(2):
             span = pl.ds(h * part, part)
-            copies.append(pltpu.make_async_copy(src.at[span], dst.at[span], sems.at[2 * i + h]))
-    for copy in copies:
-        copy.start()
-    for copy in copies:
-        copy.wait()
+            reads.append(
+                pltpu.make_async_copy(sources[i].at[span], held[i].at[span], sems.at[0, 2 * i + h])
+            )
+            writes.append(
+                pltpu.make_async_copy(held[i].at[span], results[i].at[span], sems.at[1, 2 * i + h])
+            )
+    for read in reads:
+        read.start()
+    for read, write in zip(reads, writes):
+        read.wait()
+        write.start()
+    for write in writes:
+        write.wait()
 
 
 def on_device(chunk, tile, tokens_in, grad_rows, combine_weights, live_counts, w_gate, w_up, w_down):
@@ -497,7 +505,7 @@
         out_shape=tuple(jax.ShapeDtypeStruct(a.shape, a.dtype) for a in held),
         in_specs=[anywhere] * len(held),
         out_specs=tuple([anywhere] * len(held)),
-        scratch_shapes=[dma((2 * len(held),))],
+        scratch_shapes=[vmem(a.shape, a.dtype) for a in held] + [dma((2, 2 * len(held)))],
         name="write_out",
     )(*held)
     return (

time: 200 us -> 90.8 us (0.45)
  Pallas kernels: 198 us -> 88.7 us
    pallas_call x1, Pallas kernels: 112 us -> 3.06 us  [on_device(): pl.pallas_call(functools.partial(copy_kernel, len(held)), out_shape=tuple...]
where the time goes in v4:
time: 90.8 us; the launch traced here: 89.3 us
  Pallas kernels  88.7 us (98%)
    pallas_call x1, Pallas kernels, on_device(): pl.pallas_call(functools.partial(layer_kernel, nodes, chunk, tile), out_s...  85.6 us
    pallas_call x1, Pallas kernels, on_device(): pl.pallas_call(functools.partial(copy_kernel, len(held)), out_shape=tuple...  3.06 us

profile of v4, /device:TPU:1, one launch (start us, length us, event | category | flops | bytes accessed | tf_op | source)
XLA Modules:
  0.0 89.3 jit_solution(17772550571562967551)
XLA Ops:
  0.6 85.6 %expert_backward.1 = (bf16[128,3584]{1,0:T(8,128)(2,1)}, bf16[1792,256]{1,0:T(8,128)(2,1)}, bf16[1792,256]{1,0:T(8,128)(2,1)}, bf16[1792,256]{1,0:T(8,128)(2,1)}) custom-call(bf16[1024,3584]{1,0:T(8,128)(2,1)} %bitcast.13, bf16[1024,3584]{1,0:T(8,128)(2,1)} %bitcast.14, f32[16,64]{1,0:T(8,128)} %bitcast.18, s32[1,16]{1,0:T(1,128)} %bitcast.19, ...), custom_call_target="tpu_custom_call" | custom-call | tf_op jit(solution)/shard_map/expert_backward/pallas_call | solution.py:450
  86.3 3.1 %write_out.1 = (bf16[128,3584]{1,0:T(8,128)(2,1)}, bf16[1792,256]{1,0:T(8,128)(2,1)}, bf16[1792,256]{1,0:T(8,128)(2,1)}, bf16[1792,256]{1,0:T(8,128)(2,1)}) custom-call(bf16[128,3584]{1,0:T(8,128)(2,1)} %get-tuple-element.12.refs_0_, bf16[1792,256]{1,0:T(8,128)(2,1)} %get-tuple-element.13.refs_1_, bf16[1792,256]{1,0:T(8,128)(2,1)} %get-tuple-element.14.refs_2_, ...), custom_call_target="tpu_custom_call" | custom-call | tf_op jit(solution)/shard_map/write_out/pallas_call | solution.py:503

commit v5 on v3

--- a/solution.py
+++ b/solution.py
@@ -32,8 +32,8 @@
     tok_hbm, grd_hbm, weight_ref, count_ref, wg_hbm, wu_hbm, wd_hbm,
     dtok_out, gate_out, up_out, down_out,
     tok, scl, wg, wu, wd, hid, act, actp, tok_o, act_o,
-    msend, mrecv, csum, orecv, nrecv, afin, arecv, dfin, dsend, drecv, wfin,
-    load_sem, tz_sem, az_sem, m_sem, ag_sem, fw_sem, o_sem, n_sem, a_sem, dz_sem, out_sem,
+    msend, mrecv, csum, orecv, nrecv, afin, arecv, dsend, drecv,
+    load_sem, tz_sem, az_sem, m_sem, ag_sem, fw_sem, o_sem, n_sem, a_sem, dz_sem,
 ):
     rows, width = tok.shape
     hl = wg.shape[1]
@@ -78,8 +78,6 @@
     load_wg.start()
     load_wu.start()
     tok_load(0).start()
-    load_wd.start()
-    grd_load(0).start()
 
     barrier = pltpu.get_barrier_semaphore()
     pl.semaphore_signal(barrier, inc=1, device_id={"dp": other})
@@ -109,6 +107,8 @@
 
     for p in range(RING):
         tz(p).start()
+    grd_load(0).start()
+    load_wd.start()
     tok_load(1).start()
     grd_load(1).start()
 
@@ -345,39 +345,27 @@
     for b in range(RING):
         az(b).wait_recv()
 
-    def put(which, k, out):
-        return pltpu.make_async_copy(
-            wfin.at[which, tile_rows(k)], out.at[tile_rows(k)], out_sem.at[which, k]
-        )
-
     def weights(k, carry):
         here = tile_rows(k)
         dz(k).wait_recv()
         down = dot_tn(scl[:, tile_cols(mine, k)], hid[...]).astype(BF16).astype(F32)
-        wfin[2, here, :] = (down + drecv[here, :].astype(F32)).astype(BF16)
-        put(2, k, down_out).start()
+        down_out[here, :] = (down + drecv[here, :].astype(F32)).astype(BF16)
         both = dot_tn(tok[:, tile_cols(mine, k)], act[...]) + dot_tn(
             tok_o[:, tile_cols(0, k)], act_o[...]
         )
-        wfin[0, here, :] = both[:, :hl].astype(BF16)
-        wfin[1, here, :] = both[:, hl:].astype(BF16)
-        put(0, k, gate_out).start()
-        put(1, k, up_out).start()
+        gate_out[here, :] = both[:, :hl].astype(BF16)
+        up_out[here, :] = both[:, hl:].astype(BF16)
         return carry
 
     lax.fori_loop(0, tiles, weights, 0)
 
     swap_out = swap_matrix(group, slots, nodes)
-
-    def put_rows(q):
-        cols = pl.ds(pl.multiple_of(q * chunk, chunk), chunk)
-        return pltpu.make_async_copy(dfin.at[q], dtok_out.at[:, cols], out_sem.at[3, q])
 
     def collect(q, carry):
         to_nodes(q).wait_recv()
         got = arecv[q].astype(F32).reshape(group, chunk).astype(BF16)
-        dfin[q] = jnp.dot(swap_out, got, preferred_element_type=F32).astype(BF16)
-        put_rows(q).start()
+        cols = pl.ds(pl.multiple_of(q * chunk, chunk), chunk)
+        dtok_out[:, cols] = jnp.dot(swap_out, got, preferred_element_type=F32).astype(BF16)
         return carry
 
     lax.fori_loop(0, steps, collect, 0)
@@ -397,34 +385,15 @@
             opposite(q, way).wait_send()
             neighbour(q, way).wait_send()
         to_nodes(q).wait_send()
-        put_rows(q).wait()
         return carry
 
     lax.fori_loop(0, steps, drain, 0)
 
     def drain_weights(k, carry):
         dz(k).wait_send()
-        put(0, k, gate_out).wait()
-        put(1, k, up_out).wait()
-        put(2, k, down_out).wait()
         return carry
 
     lax.fori_loop(0, tiles, drain_weights, 0)
-
-
-def copy_kernel(count, *refs):
-    sems = refs[2 * count]
-    copies = []
-    for i in range(count):
-        src, dst = refs[i], refs[count + i]
-        part = src.shape[0] // 2
-        for h in range(2):
-            span = pl.ds(h * part, part)
-            copies.append(pltpu.make_async_copy(src.at[span], dst.at[span], sems.at[2 * i + h]))
-    for copy in copies:
-        copy.start()
-    for copy in copies:
-        copy.wait()
 
 
 def on_device(chunk, tile, tokens_in, grad_rows, combine_weights, live_counts, w_gate, w_up, w_down):
@@ -438,13 +407,13 @@
     anywhere = pl.BlockSpec(memory_space=pl.ANY)
     dma = pltpu.SemaphoreType.DMA
     vmem = pltpu.VMEM
-    weight_shape = jax.ShapeDtypeStruct((half, hl), BF16)
-    held = pl.pallas_call(
+    weight_shape = vmem((half, hl), BF16)
+    d_tokens, gate, up, down = pl.pallas_call(
         functools.partial(layer_kernel, nodes, chunk, tile),
-        out_shape=(jax.ShapeDtypeStruct((group, width), BF16), weight_shape, weight_shape, weight_shape),
+        out_shape=(vmem((group, width), BF16), weight_shape, weight_shape, weight_shape),
         in_specs=[anywhere, anywhere, pl.BlockSpec(memory_space=vmem),
                   pl.BlockSpec(memory_space=vmem), anywhere, anywhere, anywhere],
-        out_specs=(anywhere, anywhere, anywhere, anywhere),
+        out_specs=tuple([pl.BlockSpec(memory_space=vmem)] * 4),
         scratch_shapes=[
             vmem((rows, width), BF16),
             vmem((rows, width), BF16),
@@ -463,10 +432,8 @@
             vmem((steps, 2, group, chunk), BF16),
             vmem((steps, nodes, group // nodes, chunk), BF16),
             vmem((steps, nodes, group // nodes, chunk), BF16),
-            vmem((steps, group, chunk), BF16),
             vmem((half, hl), BF16),
             vmem((half, hl), BF16),
-            vmem((3, half, hl), BF16),
             dma((3 + 2 * RING,)),
             dma((2, RING)),
             dma((2, RING)),
@@ -477,7 +444,6 @@
             dma((2, steps, 2)),
             dma((2, steps)),
             dma((2, tiles)),
-            dma((4, max(tiles, steps))),
         ],
         compiler_params=pltpu.CompilerParams(
             collective_id=0, has_side_effects=True, vmem_limit_bytes=VMEM_LIMIT
@@ -492,14 +458,6 @@
         w_up[0],
         w_down[0],
     )
-    d_tokens, gate, up, down = pl.pallas_call(
-        functools.partial(copy_kernel, len(held)),
-        out_shape=tuple(jax.ShapeDtypeStruct(a.shape, a.dtype) for a in held),
-        in_specs=[anywhere] * len(held),
-        out_specs=tuple([anywhere] * len(held)),
-        scratch_shapes=[dma((2 * len(held),))],
-        name="write_out",
-    )(*held)
     return (
         d_tokens.reshape(1, 1, group // nodes, nodes, width),
         gate[None],
@@ -508,7 +466,7 @@
     )
 
 
-VMEM_LIMIT = 62 * 1024 * 1024
+VMEM_LIMIT = 56 * 1024 * 1024
 CHUNK = 512
 TILE = 256
 

time: 200 us -> 90.6 us (0.45)
  Pallas kernels: 198 us -> 84.8 us
  local copies, waits for them, and re-layouts: 0 us -> 3.69 us
    pallas_call x1 -> x0, Pallas kernels: 112 us -> none  [on_device(): pl.pallas_call(functools.partial(copy_kernel, len(held)), out_shape=tuple...]
    unnamed x0 -> x4, local copies, waits for them, and re-layouts: none -> 3.69 us
where the time goes in v5:
time: 90.6 us; the launch traced here: 89.2 us
  Pallas kernels  84.8 us (94%)
  local copies, waits for them, and re-layouts  3.69 us (4%)
    pallas_call x1, Pallas kernels, on_device(): pl.pallas_call(functools.partial(layer_kernel, nodes, chunk, tile), out_s...  84.8 us
    unnamed x4, local copies, waits for them, and re-layouts  3.69 us

profile of v5, /device:TPU:1, one launch (start us, length us, event | category | flops | bytes accessed | tf_op | source)
XLA Modules:
  0.0 89.2 jit_solution(14356677599123702911)
XLA Ops:
  0.6 84.8 %expert_backward.1 = (bf16[128,3584]{1,0:T(8,128)(2,1)S(1)}, bf16[1792,256]{1,0:T(8,128)(2,1)S(1)}, bf16[1792,256]{1,0:T(8,128)(2,1)S(1)}, bf16[1792,256]{1,0:T(8,128)(2,1)S(1)}) custom-call(bf16[1024,3584]{1,0:T(8,128)(2,1)} %bitcast.17, bf16[1024,3584]{1,0:T(8,128)(2,1)} %bitcast.18, f32[16,64]{1,0:T(8,128)} %bitcast.22, s32[1,16]{1,0:T(1,128)} %bitcast.23, ...), custom_call_target="tpu_custom_call" | custom-call | tf_op jit(solution)/shard_map/expert_backward/pallas_call | solution.py:411
  85.5 0.9 %copy.15 = bf16[1,1,8,16,3584]{4,3,2,1,0:T(8,128)(2,1)} copy(bf16[1,1,8,16,3584]{4,3,2,1,0:T(8,128)(2,1)S(1)} %bitcast.16) | data formatting | bytes 1835008
  86.4 0.9 %copy.16 = bf16[1,1792,256]{2,1,0:T(8,128)(2,1)} copy(bf16[1,1792,256]{2,1,0:T(8,128)(2,1)S(1)} %bitcast.15) | data formatting | bytes 1835008
  87.3 0.9 %copy.17 = bf16[1,1792,256]{2,1,0:T(8,128)(2,1)} copy(bf16[1,1792,256]{2,1,0:T(8,128)(2,1)S(1)} %bitcast.14) | data formatting | bytes 1835008
  88.2 0.9 %copy.18 = bf16[1,1792,256]{2,1,0:T(8,128)(2,1)} copy(bf16[1,1792,256]{2,1,0:T(8,128)(2,1)S(1)} %bitcast.13) | data formatting | bytes 1835008

commit v6 on v5

--- a/solution.py
+++ b/solution.py
@@ -396,6 +396,22 @@
     lax.fori_loop(0, tiles, drain_weights, 0)
 
 
+def copy_kernel(count, *refs):
+    sources, results, sems = refs[:count], refs[count : 2 * count], refs[2 * count]
+    copies = []
+    for i in range(count):
+        part = sources[i].shape[0] // 2
+        for h in range(2):
+            span = pl.ds(h * part, part)
+            copies.append(
+                pltpu.make_async_copy(sources[i].at[span], results[i].at[span], sems.at[2 * i + h])
+            )
+    for copy in copies:
+        copy.start()
+    for copy in copies:
+        copy.wait()
+
+
 def on_device(chunk, tile, tokens_in, grad_rows, combine_weights, live_counts, w_gate, w_up, w_down):
     slot_count, nodes, width = tokens_in.shape[2:]
     rows = slot_count * nodes
@@ -408,7 +424,7 @@
     dma = pltpu.SemaphoreType.DMA
     vmem = pltpu.VMEM
     weight_shape = vmem((half, hl), BF16)
-    d_tokens, gate, up, down = pl.pallas_call(
+    held = pl.pallas_call(
         functools.partial(layer_kernel, nodes, chunk, tile),
         out_shape=(vmem((group, width), BF16), weight_shape, weight_shape, weight_shape),
         in_specs=[anywhere, anywhere, pl.BlockSpec(memory_space=vmem),
@@ -458,6 +474,16 @@
         w_up[0],
         w_down[0],
     )
+    held = [pltpu.with_memory_space_constraint(a, vmem) for a in held]
+    d_tokens, gate, up, down = pl.pallas_call(
+        functools.partial(copy_kernel, len(held)),
+        out_shape=tuple(jax.ShapeDtypeStruct(a.shape, a.dtype) for a in held),
+        in_specs=[pl.BlockSpec(memory_space=vmem)] * len(held),
+        out_specs=tuple([anywhere] * len(held)),
+        scratch_shapes=[dma((2 * len(held),))],
+        compiler_params=pltpu.CompilerParams(vmem_limit_bytes=1024 * 1024),
+        name="write_out",
+    )(*held)
     return (
         d_tokens.reshape(1, 1, group // nodes, nodes, width),
         gate[None],

time: 90.6 us -> 88.8 us (0.980)
  local copies, waits for them, and re-layouts: 3.69 us -> 0 us
  Pallas kernels: 84.8 us -> 86.7 us
    unnamed x4 -> x0, local copies, waits for them, and re-layouts: 3.69 us -> none
    pallas_call x0 -> x1, Pallas kernels: none -> 1.9 us  [on_device(): pl.pallas_call(functools.partial(copy_kernel, len(held)), out_shape=tuple...]
where the time goes in v6:
time: 88.8 us; the launch traced here: 87.4 us
  Pallas kernels  86.7 us (98%)
    pallas_call x1, Pallas kernels, on_device(): pl.pallas_call(functools.partial(layer_kernel, nodes, chunk, tile), out_s...  84.8 us
    pallas_call x1, Pallas kernels, on_device(): pl.pallas_call(functools.partial(copy_kernel, len(held)), out_shape=tuple...  1.9 us

profile of v6, /device:TPU:1, one launch (start us, length us, event | category | flops | bytes accessed | tf_op | source)
XLA Modules:
  0.0 87.4 jit_solution(17362549176795018629)
XLA Ops:
  0.6 84.8 %expert_backward.1 = (bf16[128,3584]{1,0:T(8,128)(2,1)S(1)}, bf16[1792,256]{1,0:T(8,128)(2,1)S(1)}, bf16[1792,256]{1,0:T(8,128)(2,1)S(1)}, bf16[1792,256]{1,0:T(8,128)(2,1)S(1)}) custom-call(bf16[1024,3584]{1,0:T(8,128)(2,1)} %bitcast.13, bf16[1024,3584]{1,0:T(8,128)(2,1)} %bitcast.14, f32[16,64]{1,0:T(8,128)} %bitcast.18, s32[1,16]{1,0:T(1,128)} %bitcast.19, ...), custom_call_target="tpu_custom_call" | custom-call | tf_op jit(solution)/shard_map/expert_backward/pallas_call | solution.py:427
  85.5 1.9 %write_out.1 = (bf16[128,3584]{1,0:T(8,128)(2,1)}, bf16[1792,256]{1,0:T(8,128)(2,1)}, bf16[1792,256]{1,0:T(8,128)(2,1)}, bf16[1792,256]{1,0:T(8,128)(2,1)}) custom-call(bf16[128,3584]{1,0:T(8,128)(2,1)S(1)} %get-tuple-element.12.refs_0_, bf16[1792,256]{1,0:T(8,128)(2,1)S(1)} %get-tuple-element.13.refs_1_, bf16[1792,256]{1,0:T(8,128)(2,1)S(1)} %get-tuple-element.14.refs_2_, ...), custom_call_target="tpu_custom_call" | custom-call | tf_op jit(solution)/shard_map/write_out/pallas_call | solution.py:478

commit v7 on v6

--- a/solution.py
+++ b/solution.py
@@ -75,9 +75,6 @@
     load_wg = load(wg_hbm, wg, 0)
     load_wu = load(wu_hbm, wu, 1)
     load_wd = load(wd_hbm, wd, 2)
-    load_wg.start()
-    load_wu.start()
-    tok_load(0).start()
 
     barrier = pltpu.get_barrier_semaphore()
     pl.semaphore_signal(barrier, inc=1, device_id={"dp": other})
@@ -90,6 +87,9 @@
         return carry
 
     lax.fori_loop(1, nodes, greet, 0)
+    load_wg.start()
+    load_wu.start()
+    tok_load(0).start()
     pl.semaphore_wait(barrier, 2 + RING - 1 + nodes - 1)
 
     def group_rows(l):
@@ -359,17 +359,6 @@
 
     lax.fori_loop(0, tiles, weights, 0)
 
-    swap_out = swap_matrix(group, slots, nodes)
-
-    def collect(q, carry):
-        to_nodes(q).wait_recv()
-        got = arecv[q].astype(F32).reshape(group, chunk).astype(BF16)
-        cols = pl.ds(pl.multiple_of(q * chunk, chunk), chunk)
-        dtok_out[:, cols] = jnp.dot(swap_out, got, preferred_element_type=F32).astype(BF16)
-        return carry
-
-    lax.fori_loop(0, steps, collect, 0)
-
     for b in range(RING):
         tz(b).wait_send()
         az(b).wait_send()
@@ -384,7 +373,6 @@
         for way in range(2):
             opposite(q, way).wait_send()
             neighbour(q, way).wait_send()
-        to_nodes(q).wait_send()
         return carry
 
     lax.fori_loop(0, steps, drain, 0)
@@ -394,6 +382,18 @@
         return carry
 
     lax.fori_loop(0, tiles, drain_weights, 0)
+
+    swap_out = swap_matrix(group, slots, nodes)
+
+    def collect(q, carry):
+        to_nodes(q).wait_recv()
+        got = arecv[q].astype(F32).reshape(group, chunk).astype(BF16)
+        cols = pl.ds(pl.multiple_of(q * chunk, chunk), chunk)
+        dtok_out[:, cols] = jnp.dot(swap_out, got, preferred_element_type=F32).astype(BF16)
+        to_nodes(q).wait_send()
+        return carry
+
+    lax.fori_loop(0, steps, collect, 0)
 
 
 def copy_kernel(count, *refs):

time: 88.8 us -> 88.6 us (level)
  no operation moved by 1% of the time
where the time goes in v7:
time: 88.6 us; the launch traced here: 87.2 us
  Pallas kernels  86.6 us (98%)
    pallas_call x1, Pallas kernels, on_device(): pl.pallas_call(functools.partial(layer_kernel, nodes, chunk, tile), out_s...  84.7 us
    pallas_call x1, Pallas kernels, on_device(): pl.pallas_call(functools.partial(copy_kernel, len(held)), out_shape=tuple...  1.9 us

profile of v7, /device:TPU:1, one launch (start us, length us, event | category | flops | bytes accessed | tf_op | source)
XLA Modules:
  0.0 87.2 jit_solution(12973838850705698816)
XLA Ops:
  0.6 84.7 %expert_backward.1 = (bf16[128,3584]{1,0:T(8,128)(2,1)S(1)}, bf16[1792,256]{1,0:T(8,128)(2,1)S(1)}, bf16[1792,256]{1,0:T(8,128)(2,1)S(1)}, bf16[1792,256]{1,0:T(8,128)(2,1)S(1)}) custom-call(bf16[1024,3584]{1,0:T(8,128)(2,1)} %bitcast.13, bf16[1024,3584]{1,0:T(8,128)(2,1)} %bitcast.14, f32[16,64]{1,0:T(8,128)} %bitcast.18, s32[1,16]{1,0:T(1,128)} %bitcast.19, ...), custom_call_target="tpu_custom_call" | custom-call | tf_op jit(solution)/shard_map/expert_backward/pallas_call | solution.py:427
  85.3 1.9 %write_out.1 = (bf16[128,3584]{1,0:T(8,128)(2,1)}, bf16[1792,256]{1,0:T(8,128)(2,1)}, bf16[1792,256]{1,0:T(8,128)(2,1)}, bf16[1792,256]{1,0:T(8,128)(2,1)}) custom-call(bf16[128,3584]{1,0:T(8,128)(2,1)S(1)} %get-tuple-element.12.refs_0_, bf16[1792,256]{1,0:T(8,128)(2,1)S(1)} %get-tuple-element.13.refs_1_, bf16[1792,256]{1,0:T(8,128)(2,1)S(1)} %get-tuple-element.14.refs_2_, ...), custom_call_target="tpu_custom_call" | custom-call | tf_op jit(solution)/shard_map/write_out/pallas_call | solution.py:478

commit v8 on v6

--- a/solution.py
+++ b/solution.py
@@ -109,8 +109,6 @@
         tz(p).start()
     grd_load(0).start()
     load_wd.start()
-    tok_load(1).start()
-    grd_load(1).start()
 
     def spread(step, p):
         return pltpu.make_async_remote_copy(
@@ -155,10 +153,10 @@
         def _():
             load_wd.wait()
 
-        @pl.when(b < RING - 2)
-        def _():
-            tok_load(b + 2).start()
-            grd_load(b + 2).start()
+        @pl.when(b < RING - 1)
+        def _():
+            tok_load(b + 1).start()
+            grd_load(b + 1).start()
 
         scale = jnp.sum(
             jnp.where(slot_lane == row_slot + b * (block // nodes), row_weights, 0.0),

time: 88.8 us -> 88.8 us (level)
  no operation moved by 1% of the time
where the time goes in v8:
time: 88.8 us; the launch traced here: 87.4 us
  Pallas kernels  86.7 us (98%)
    pallas_call x1, Pallas kernels, on_device(): pl.pallas_call(functools.partial(layer_kernel, nodes, chunk, tile), out_s...  84.8 us
    pallas_call x1, Pallas kernels, on_device(): pl.pallas_call(functools.partial(copy_kernel, len(held)), out_shape=tuple...  1.9 us

profile of v8, /device:TPU:1, one launch (start us, length us, event | category | flops | bytes accessed | tf_op | source)
XLA Modules:
  0.0 87.4 jit_solution(14607162437147701363)
XLA Ops:
  0.6 84.8 %expert_backward.1 = (bf16[128,3584]{1,0:T(8,128)(2,1)S(1)}, bf16[1792,256]{1,0:T(8,128)(2,1)S(1)}, bf16[1792,256]{1,0:T(8,128)(2,1)S(1)}, bf16[1792,256]{1,0:T(8,128)(2,1)S(1)}) custom-call(bf16[1024,3584]{1,0:T(8,128)(2,1)} %bitcast.13, bf16[1024,3584]{1,0:T(8,128)(2,1)} %bitcast.14, f32[16,64]{1,0:T(8,128)} %bitcast.18, s32[1,16]{1,0:T(1,128)} %bitcast.19, ...), custom_call_target="tpu_custom_call" | custom-call | tf_op jit(solution)/shard_map/expert_backward/pallas_call | solution.py:425
  85.5 1.9 %write_out.1 = (bf16[128,3584]{1,0:T(8,128)(2,1)}, bf16[1792,256]{1,0:T(8,128)(2,1)}, bf16[1792,256]{1,0:T(8,128)(2,1)}, bf16[1792,256]{1,0:T(8,128)(2,1)}) custom-call(bf16[128,3584]{1,0:T(8,128)(2,1)S(1)} %get-tuple-element.12.refs_0_, bf16[1792,256]{1,0:T(8,128)(2,1)S(1)} %get-tuple-element.13.refs_1_, bf16[1792,256]{1,0:T(8,128)(2,1)S(1)} %get-tuple-element.14.refs_2_, ...), custom_call_target="tpu_custom_call" | custom-call | tf_op jit(solution)/shard_map/write_out/pallas_call | solution.py:476
